TPU v7x, 32 devices: a whole 2x2x4 slice. The times are simulated.
32 devices in a mesh: wealth: 4 (over z), income: 8 (over y, x, core).
Axes of the slice: x: 2, y: 2, z: 4, core: 2. Of those that a mesh axis runs over, the one named last changes fastest.
Arguments:
- value_field: float32 [8192, 4096], P('income', 'wealth'), may hold values from -4.5 to 4.5
- income: float32 [8192], P('income'), may hold values from 0.5 to 2
- jump_rates: float32 [8192, 8192], P(None, 'income'), may hold values from 0 to 0.024414062, as said below
Outputs:
- value_next: float32 [8192, 4096], P('income', 'wealth')
Inputs may be any that keep to these rules, and one draw needn't show every extreme that they name: jump_rates is symmetric, with nonnegative entries.
All inputs are finite; a program needn't handle non-finite values.
Results may differ from a plain program's by a relative error of at most 0.000057.
Values sent between devices are 32-bit elements; how exact they have to be, the bound alone decides.
No kernel may reach another device: no remote copies, remote signals or barrier semaphores. Data moves between devices by JAX's collectives and lax.ppermute only.
A program may use at most 192 MiB of HBM per device.

v0:
```python
import jax
import jax.numpy as jnp
from jax import lax
from jax.sharding import PartitionSpec as P

interest = 0.03
premium = 0.3
volatility = 0.5
discount = 0.05
time_step = 0.5
slope_floor = 0.2


def with_halo(shard, sides, width):
    for axis, dim in sides:
        count, length = (lax.axis_size(axis), shard.shape[dim])
        up = [(i, (i + 1) % count) for i in range(count - 1)]
        down = [(j, i) for i, j in up]
        last = lax.slice_in_dim(shard, length - width, length, axis=dim)
        first = lax.slice_in_dim(shard, 0, width, axis=dim)
        before = lax.ppermute(last, axis, up)
        after = lax.ppermute(first, axis, down)
        shard = jnp.concatenate([before, shard, after], axis=dim)
    return shard


def hamiltonian(padded, income, wealth_grid):
    step_up = padded[:, 2:] - padded[:, 1:-1]
    step_down = padded[:, 1:-1] - padded[:, :-2]
    gradient = 0.5 * (step_up + step_down)
    curvature = step_up - step_down
    clipped = jnp.maximum(gradient, slope_floor)
    consumption = 1.0 / clipped
    concave = jnp.maximum(-curvature, 1.0)
    risky_share = jnp.clip(
        premium * gradient / (volatility * volatility * wealth_grid[None, :] * concave), 0.0, 1.0
    )
    exposure = risky_share * wealth_grid[None, :]
    drift_term = income[:, None] + interest * wealth_grid[None, :] - consumption
    return (
        -jnp.log(clipped)
        + gradient * drift_term
        + premium * exposure * gradient
        + 0.5 * volatility * volatility * exposure * exposure * curvature
    )


def local(value_field, income, jump_rates):
    slab_rows, slab_cols = value_field.shape
    wealth_count = lax.axis_size("wealth")
    wealth_index = lax.axis_index("wealth")
    outflow = jnp.sum(jump_rates, axis=0)
    jump_terms = lax.psum_scatter(
        jnp.dot(
            jump_rates,
            value_field,
            precision=lax.Precision.HIGHEST,
            preferred_element_type=jnp.float32,
        ),
        "income",
        scatter_dimension=0,
        tiled=True,
    )
    extended = with_halo(value_field, (("wealth", 1),), 1)
    lower_edge = jnp.where(wealth_index == 0, value_field[:, 0] - 1.0 / income, extended[:, 0])
    upper_edge = jnp.where(wealth_index == wealth_count - 1, value_field[:, -1], extended[:, -1])
    padded = jnp.concatenate([lower_edge[:, None], value_field, upper_edge[:, None]], axis=1)
    wealth_grid = (wealth_index * slab_cols + jnp.arange(slab_cols) + 1).astype(jnp.float32) / (
        slab_cols * wealth_count
    )
    local_part = hamiltonian(padded, income, wealth_grid)
    change = local_part + jump_terms - (outflow[:, None] + discount) * value_field
    return value_field + time_step * change


def solution(mesh):
    return jax.shard_map(
        local,
        mesh=mesh,
        in_specs=(P("income", "wealth"), P("income"), P(None, "income")),
        out_specs=P("income", "wealth"),
        check_vma=False,
    )
```

profile of v0, /device:TPU:0, one launch (start us, length us, event | category | flops | bytes accessed | tf_op | source)
XLA Modules:
  0.0 349.1 jit_solution(17203635841033302191)
XLA Ops:
  6.5 0.0 reduce-scatter.2.cloned.1.call-start
  6.5 114.5 %fusion.8 = f32[8192,1024]{1,0:T(8,128)} fusion(f32[8192,1024]{1,0:T(8,128)} %param.5, f32[1024,1024]{1,0:T(8,128)} %param.3), kind=kOutput, calls=%fused_computation.20 | convolution fusion | flops 103079215104 | bytes 71303168 | tf_op jit(solution)/shard_map/dot_general | solution.py:54
  121.0 0.0 reduce-scatter.2.cloned.1.call-update
  121.0 1.1 slice.17
  122.1 1.3 collective-permute-start
  123.4 0.0 copy-start
  123.4 17.2 %reduce_sum.9 = f32[1024]{0:T(1024)S(1)} reduce(f32[8192,1024]{1,0:T(8,128)} %param.5, f32[]{:T(128)} %constant.13.clone.1), dimensions={0}, to_apply=%region_1.0 | reduce | flops 8387584 | bytes 33558532 | tf_op jit(solution)/shard_map/reduce_sum | solution.py:52
  140.6 0.0 collective-permute-done
  140.7 1.7 slice_reduce_fusion
  142.4 6.1 %collective-permute-start.1 = (f32[1024,1]{1,0:T(8,128)S(1)}, f32[1024,1]{1,0:T(8,128)S(1)}, u32[]{:S(2)}, u32[]{:S(2)}) collective-permute-start(f32[1024,1]{1,0:T(8,128)S(1)} %get-tuple-element.7), channel_id=1, source_target_pairs={{0,8},{8,16},{16,24},{1,9},{9,17},{17,25},{2,10},{10,18},{18,26},{... | collective-permute-start | bytes 12296 | tf_op jit(solution)/shard_map/ppermute | solution.py:21
  148.5 11.2 %collective-permute-done.1 = f32[1024,1]{1,0:T(8,128)S(1)} collective-permute-done((f32[1024,1]{1,0:T(8,128)S(1)}, f32[1024,1]{1,0:T(8,128)S(1)}, u32[]{:S(2)}, u32[]{:S(2)}) %collective-permute-start.1) | collective-permute-done | bytes 4128 | tf_op jit(solution)/shard_map/ppermute | solution.py:21
  159.7 0.2 reduce.1
  159.9 0.0 copy-done
  159.9 0.2 copy.4
  160.2 169.3 %reduce-scatter.2.cloned.1.call-done = f32[1024,1024]{1,0:T(8,128)} async-done(((f32[8192,1024]{1,0:T(8,128)}), f32[1024,1024]{1,0:T(8,128)}) %reduce-scatter.2.cloned.1.call-update) | async-done | bytes 4194320 | tf_op jit(solution)/shard_map/reduce_scatter | solution.py:53
  329.4 12.8 %fusion.5 = f32[1024,1024]{1,0:T(8,128)} fusion(f32[1024,1024]{1,0:T(8,128)} %param.3, f32[1024,1024]{1,0:T(8,128)} %reduce-scatter.2.cloned.1.call-done, f32[1024,1]{1,0:T(8,128)S(1)} %get-tuple-element.6, f32[1024,1]{1,0:T(8,128)S(1)} %copy.4, f32[1024]{0:T(1024)S(1)} %broadcast_add_fusion, f32[1024]{0:T(1024)S(1)} %get-tuple-element.8, ...), kind=kLoop, calls=%fused_computation.6 | loop fusion | flops 34603008 | bytes 12611584 | tf_op jit(solution)/shard_map/add | solution.py:73
  (4 shorter events, 0.0 us)
Async XLA Ops:
  6.5 322.9 %reduce-scatter.2.cloned.1.call-start = ((), (), s32[]{:S(2)}) async-start(), calls=%async_computation.1 | async-start | bytes 37748736 | tf_op jit(solution)/shard_map/reduce_scatter | solution.py:53
  122.1 18.5 %collective-permute-start = (f32[1024,1]{1,0:T(8,128)S(1)}, f32[1024,1]{1,0:T(8,128)S(1)}, u32[]{:S(2)}, u32[]{:S(2)}) collective-permute-start(f32[1024,1]{1,0:T(8,128)S(1)} %slice.17), channel_id=1, source_target_pairs={{8,0},{16,8},{24,16},{9,1},{17,9},{25,17},{10,2},{18,10},{26,18},{... | collective-permute-start | bytes 12296 | tf_op jit(solution)/shard_map/ppermute | solution.py:22
  123.4 36.5 %copy-start = (f32[1024]{0:T(1024)S(1)}, f32[1024]{0:T(1024)}, u32[]{:S(2)}) copy-start(f32[1024]{0:T(1024)} %param.4) | copy-start | bytes 12292
  142.4 17.3 %collective-permute-start.1 = (f32[1024,1]{1,0:T(8,128)S(1)}, f32[1024,1]{1,0:T(8,128)S(1)}, u32[]{:S(2)}, u32[]{:S(2)}) collective-permute-start(f32[1024,1]{1,0:T(8,128)S(1)} %get-tuple-element.7), channel_id=1, source_target_pairs={{0,8},{8,16},{16,24},{1,9},{9,17},{17,25},{2,10},{10,18},{18,26},{... | collective-permute-start | bytes 12296 | tf_op jit(solution)/shard_map/ppermute | solution.py:21
Sparse Core Ops, SparseCore 0:
  121.2 208.2 reduce-scatter.1
where the time goes:
time: 349 us
  waiting for transfers between devices  180 us (52%)
  matrix products  114 us (33%)
  other arithmetic  31.9 us (9%)
  between operations  13.5 us (4%)
  starting transfers between devices  7.37 us (2%)
    reduce_scatter x1, waiting for transfers between devices, local(): lax.psum_scatter(jnp.dot(jump_rates, value_field, precision=lax.Precision...  169 us
    dot_general x1, matrix products, local(): jnp.dot(jump_rates, value_field, precision=lax.Precision.HIGHEST, preferr...  114 us
    reduce_sum x1, other arithmetic, local(): outflow = jnp.sum(jump_rates, axis=0)  17.2 us
    add x1, other arithmetic, local(): return value_field + time_step * change  12.8 us
    ppermute x1, waiting for transfers between devices, with_halo(): before = lax.ppermute(last, axis, up)  11.2 us
  transfers between devices with their start and end apart: 3, of which 2 were waited for; matrix products, arithmetic and copies ran while one was open for 6% of the time, Pallas kernels for 0%

commit v1 on v0

v1 whole, which is shorter than its diff:
```python
import jax
import jax.numpy as jnp
from jax import lax
from jax.experimental import pallas as pl
from jax.experimental.pallas import tpu as pltpu
from jax.sharding import PartitionSpec as P


interest = 0.03
premium = 0.3
volatility = 0.5
discount = 0.05
time_step = 0.5
slope_floor = 0.2


def hamiltonian(padded, income, wealth_grid):
    step_up = padded[:, 2:] - padded[:, 1:-1]
    step_down = padded[:, 1:-1] - padded[:, :-2]
    gradient = 0.5 * (step_up + step_down)
    curvature = step_up - step_down
    clipped = jnp.maximum(gradient, slope_floor)
    consumption = 1.0 / clipped
    concave = jnp.maximum(-curvature, 1.0)
    risky_share = jnp.clip(
        premium * gradient / (volatility * volatility * wealth_grid[None, :] * concave), 0.0, 1.0
    )
    exposure = risky_share * wealth_grid[None, :]
    drift_term = income[:, None] + interest * wealth_grid[None, :] - consumption
    return (
        -jnp.log(clipped)
        + gradient * drift_term
        + premium * exposure * gradient
        + 0.5 * volatility * volatility * exposure * exposure * curvature
    )


def base_part(value_field, income, outflow):
    slab_cols = value_field.shape[1]
    count = lax.axis_size("wealth")
    index = lax.axis_index("wealth")
    up = [(i, i + 1) for i in range(count - 1)]
    down = [(j, i) for i, j in up]
    before = lax.ppermute(value_field[:, -1], "wealth", up)
    after = lax.ppermute(value_field[:, 0], "wealth", down)
    lower_edge = jnp.where(index == 0, value_field[:, 0] - 1.0 / income, before)
    upper_edge = jnp.where(index == count - 1, value_field[:, -1], after)
    padded = jnp.concatenate([lower_edge[:, None], value_field, upper_edge[:, None]], axis=1)
    wealth_grid = (index * slab_cols + jnp.arange(slab_cols) + 1).astype(jnp.float32) / (
        slab_cols * count
    )
    local_part = hamiltonian(padded, income, wealth_grid)
    return value_field + time_step * (local_part - (outflow[:, None] + discount) * value_field)


def split(a):
    high = a.astype(jnp.bfloat16)
    return high, (a - high.astype(jnp.float32)).astype(jnp.bfloat16)


def dot_cols(a, b):
    return jnp.dot(a, b, preferred_element_type=jnp.float32)


def dot_rows(a, b):
    return lax.dot_general(a, b, (((0,), (0,)), ((), ())), preferred_element_type=jnp.float32)


def add_jumps(total, rates, me, pieces, cols, tile=256):
    rows, width = total.shape
    count = len(pieces)
    values = [p for p, _, _ in pieces]
    depth = sum(p.shape[0] for p in values)

    def body(at, *refs):
        value, rate = refs[:count], refs[count : 2 * count]
        old, new, high, low = refs[2 * count :]

        @pl.when(pl.program_id(0) == 0)
        def _():
            first = 0
            for ref in value:
                last = first + ref.shape[0]
                high[first:last], low[first:last] = split(ref[...])
                first = last

        rate_high, rate_low = split(jnp.concatenate([ref[...] for ref in rate], axis=0))
        acc = dot_rows(rate_low, high[...]) + dot_rows(rate_high, low[...])
        new[...] = old[...] + time_step * (dot_rows(rate_high, high[...]) + acc)

    def rate_block(p, bits, first):
        size = p.shape[0]
        return pl.BlockSpec(
            (size, tile), lambda m, at: ((at[0] ^ bits) * (rows // size) + first // size, m)
        )

    specs = [pl.BlockSpec((p.shape[0], cols), lambda m, at: (0, 0)) for p in values]
    specs += [rate_block(*piece) for piece in pieces]
    specs += [pl.BlockSpec((tile, cols), lambda m, at: (m, 0))]
    return pl.pallas_call(
        body,
        out_shape=jax.ShapeDtypeStruct((rows, width), jnp.float32),
        grid_spec=pltpu.PrefetchScalarGridSpec(
            num_scalar_prefetch=1,
            grid=(rows // tile,),
            in_specs=specs,
            out_specs=pl.BlockSpec((tile, cols), lambda m, at: (m, 0)),
            scratch_shapes=[pltpu.VMEM((depth, cols), jnp.bfloat16)] * 2,
        ),
        input_output_aliases={1 + 2 * count: 0},
        cost_estimate=pl.CostEstimate(
            flops=6 * rows * cols * depth,
            bytes_accessed=8 * rows * cols + 4 * depth * (rows + cols),
            transcendentals=0,
        ),
        name="add_jumps",
    )(me.reshape(1), *values, *([rates] * count), total)


def partial_jumps(value_field, rates, me, bit, wide, tile=512):
    rows, cols = value_field.shape
    steps = rows // tile

    def body(at, value, rate, part, sums, high, low):
        first = (pl.program_id(0) == 0) & (pl.program_id(1) == 0)

        @pl.when(first)
        def _():
            high[...], low[...] = split(value[...])
            sums[...] = jnp.zeros_like(sums)

        block = rate[...]
        sums[...] += jnp.sum(block.reshape(tile // 8, 8, rows), axis=0)
        rate_high, rate_low = split(block)
        acc = dot_cols(rate_low, high[...]) + dot_cols(rate_high, low[...])
        part[...] = (dot_cols(rate_high, high[...]) + acc)[None]

    return pl.pallas_call(
        body,
        out_shape=(
            jax.ShapeDtypeStruct((4, rows, wide), jnp.float32),
            jax.ShapeDtypeStruct((8, rows), jnp.float32),
        ),
        grid_spec=pltpu.PrefetchScalarGridSpec(
            num_scalar_prefetch=1,
            grid=(4, steps),
            in_specs=[
                pl.BlockSpec((rows, wide), lambda q, m, at: (0, cols // wide - 1)),
                pl.BlockSpec((tile, rows), lambda q, m, at: ((at[0] ^ bit ^ (2 * q)) * steps + m, 0)),
            ],
            out_specs=(
                pl.BlockSpec((1, tile, wide), lambda q, m, at: (q, m, 0)),
                pl.BlockSpec((8, rows), lambda q, m, at: (0, 0)),
            ),
            scratch_shapes=[pltpu.VMEM((rows, wide), jnp.bfloat16)] * 2,
        ),
        cost_estimate=pl.CostEstimate(
            flops=24 * rows * rows * wide, bytes_accessed=16 * rows * (rows + 2 * wide), transcendentals=0
        ),
        name="partial_jumps",
    )(me.reshape(1), value_field, rates)


def add_last(total, plain, combined, own):
    rows, cols = total.shape
    half, wide = plain[0].shape

    def body(plain_a, plain_b, combined_a, combined_b, own_part, old, new):
        new[:half] = old[:half] + time_step * (own_part[:half] + plain_a[...] + combined_a[...])
        new[half:] = old[half:] + time_step * (own_part[half:] + plain_b[...] + combined_b[...])

    part = pl.BlockSpec((half, wide), lambda m: (0, 0))
    whole = pl.BlockSpec((rows, wide), lambda m: (0, 0))
    last = pl.BlockSpec((rows, wide), lambda m: (0, cols // wide - 1))
    return pl.pallas_call(
        body,
        grid=(1,),
        out_shape=jax.ShapeDtypeStruct((rows, cols), jnp.float32),
        in_specs=[part] * 4 + [whole, last],
        out_specs=last,
        input_output_aliases={5: 0},
        name="add_last",
    )(*plain, *combined, own, total)


def swap(x, bit):
    count = lax.axis_size("income")
    return lax.ppermute(x, "income", [(i, i ^ bit) for i in range(count)])


def local_grid(value_field, income, jump_rates):
    return step_grid(value_field, income, jump_rates)


def step_grid(value_field, income, jump_rates):
    rows, cols = value_field.shape
    half, wide = rows // 2, cols // 4
    narrow = cols - wide
    me = lax.axis_index("income")

    def add(total, items):
        return add_jumps(total, jump_rates, me, items, narrow)

    def both(v, bits, first):
        return [(v, bits, first), (swap(v, 1), bits ^ 1, first)]

    half_a, half_b = value_field[:half, :narrow], value_field[half:, :narrow]
    x_a, y_b = swap(half_a, 2), swap(half_b, 4)
    x_b, y_a = swap(half_b, 2), swap(half_a, 4)
    far_a, far_b = swap(x_a, 4), swap(y_b, 2)
    other = swap(value_field, 1)

    send, sums_send = partial_jumps(value_field, jump_rates, me, 1, wide)
    keep, sums_keep = partial_jumps(value_field, jump_rates, me, 0, wide)
    got = swap(send, 1)

    def parts(q, first):
        return keep[q, first : first + half] + got[q, first : first + half]

    first_x = swap(parts(3, 0), 2)
    first_y = swap(parts(3, half), 4)
    plain_x = swap(parts(1, 0), 2)
    plain_y = swap(parts(2, half), 4)
    comb_x = swap(parts(1, half) + first_y, 2)
    comb_y = swap(parts(2, 0) + first_x, 4)

    outflow = jnp.sum(sums_send + sums_keep, axis=0)
    total = base_part(value_field, income, outflow)
    total = add(total, [(value_field, 0, 0), (other, 1, 0)])
    total = add(total, both(x_a, 2, 0) + both(y_b, 4, half))
    total = add(total, both(x_b, 2, half) + both(y_a, 4, 0))
    total = add(total, both(far_a, 6, 0) + both(far_b, 6, half))
    return add_last(total, (plain_x, plain_y), (comb_y, comb_x), keep[0] + got[0])


def local_any(value_field, income, jump_rates):
    jump_terms = lax.psum_scatter(
        jnp.dot(
            jump_rates,
            value_field,
            precision=lax.Precision.HIGHEST,
            preferred_element_type=jnp.float32,
        ),
        "income",
        scatter_dimension=0,
        tiled=True,
    )
    outflow = jnp.sum(jump_rates, axis=0)
    return base_part(value_field, income, outflow) + time_step * jump_terms


def solution(mesh):
    grid = mesh.shape["income"] == 8
    return jax.shard_map(
        local_grid if grid else local_any,
        mesh=mesh,
        in_specs=(P("income", "wealth"), P("income"), P(None, "income")),
        out_specs=P("income", "wealth"),
        check_vma=False,
    )
```

time: 349 us -> 204 us (0.58)
  waiting for transfers between devices: 180 us -> 53.2 us
  matrix products: 114 us -> 0 us
  Pallas kernels: 0 us -> 97 us
  starting transfers between devices: 7.37 us -> 22.5 us
  between operations: 13.5 us -> 0.15 us
  other arithmetic: 31.9 us -> 21 us
  local copies, waits for them, and re-layouts: 1.31 us -> 9.04 us
    reduce_scatter x1 -> x0, waiting for transfers between devices: 169 us -> none  [local(): lax.psum_scatter(jnp.dot(jump_rates, value_field, precision=lax.Precision...]
    dot_general x1 -> x0, matrix products: 114 us -> none  [local(): jnp.dot(jump_rates, value_field, precision=lax.Precision.HIGHEST, preferr...]
    pallas_call x0 -> x7, Pallas kernels: none -> 97 us  [the longest x4 66.3 us: add_jumps(): pl.pallas_call(body, out_shape=jax.ShapeDtypeStruct((rows, width), jnp.fl...]
    ppermute x2 -> x22, waiting for transfers between devices: 11.2 us -> 53.2 us  [the longest x20 50.6 us: swap(): return lax.ppermute(x, 'income', [(i, i ^ bit) for i in range(count)])]
    reduce_sum x1, other arithmetic: 17.2 us -> 0.77 us  [step_grid(): outflow = jnp.sum(sums_send + sums_keep, axis=0)]
    ppermute x2 -> x22, starting transfers between devices: 7.37 us -> 22.5 us  [the longest x20 17.7 us: swap(): return lax.ppermute(x, 'income', [(i, i ^ bit) for i in range(count)])]
    add x2 -> x4, other arithmetic: 12.8 us -> 20.2 us  [the longest x1 11.7 us: base_part(): value_field + time_step * (local_part - (outflow[:, None] + discount) * v...]
    slice x1 -> x2, local copies, waits for them, and re-layouts: 1.08 us -> 5.44 us  [the longest x1 3.74 us: step_grid(): half_a, half_b = (value_field[:half, :narrow], value_field[half:, :narrow])]
  transfers between devices with their start and end apart: 3 -> 22, of which waited for: 2 -> 6; matrix products, arithmetic and copies ran while one was open for 6% -> 13% of each run, Pallas kernels for 0% -> 39%
where the time goes in v1:
time: 204 us; the launch traced here: 203 us
  Pallas kernels  97 us (48%)
  waiting for transfers between devices  53.2 us (26%)
  starting transfers between devices  22.5 us (11%)
  other arithmetic  21 us (10%)
  local copies, waits for them, and re-layouts  9.04 us (4%)
    pallas_call x4, Pallas kernels, add_jumps(): pl.pallas_call(body, out_shape=jax.ShapeDtypeStruct((rows, width), jnp.fl...  66.3 us
    ppermute x20, waiting for transfers between devices, swap(): return lax.ppermute(x, 'income', [(i, i ^ bit) for i in range(count)])  50.6 us
    pallas_call x2, Pallas kernels, partial_jumps(): pl.pallas_call(body, out_shape=(jax.ShapeDtypeStruct((4, rows, wide), jnp...  27.3 us
    ppermute x20, starting transfers between devices, swap(): return lax.ppermute(x, 'income', [(i, i ^ bit) for i in range(count)])  17.7 us
    add x1, other arithmetic, base_part(): value_field + time_step * (local_part - (outflow[:, None] + discount) * v...  11.7 us
  transfers between devices with their start and end apart: 22, of which 6 were waited for; matrix products, arithmetic and copies ran while one was open for 13% of the time, Pallas kernels for 39%

profile of v1, /device:TPU:0, one launch (start us, length us, event | category | flops | bytes accessed | tf_op | source)
XLA Modules:
  0.0 202.8 jit_solution(12640096088406973401)
XLA Ops:
  0.0 13.6 %partial_jumps.3 = (f32[4,1024,256]{2,1,0:T(8,128)}, f32[8,1024]{1,0:T(8,128)}) custom-call(s32[1]{0:T(128)} %bitcast.at, f32[1024,1024]{1,0:T(8,128)} %refs_0_.1, f32[8192,1024]{1,0:T(8,128)} %refs_7_.5), custom_call_target="tpu_custom_call" | custom-call | flops 6442450944 | bytes 25165824 | tf_op jit(solution)/shard_map/partial_jumps/pallas_call | solution.py:138
  14.1 3.7 %fusion.16 = (f32[512,768]{1,0:T(8,128)}, f32[512,768]{1,0:T(8,128)}) fusion(f32[1024,1024]{1,0:T(8,128)} %refs_0_.1), kind=kLoop, calls=%fused_computation.37 | loop fusion | bytes 6291456 | tf_op jit(solution)/shard_map/slice | solution.py:207
  17.9 2.5 %collective-permute-start.7 = (f32[512,768]{1,0:T(8,128)}, f32[512,768]{1,0:T(8,128)S(1)}, u32[]{:S(2)}, u32[]{:S(2)}) collective-permute-start(f32[512,768]{1,0:T(8,128)} %get-tuple-element.22), channel_id=1, source_target_pairs={{0,2},{1,3},{2,0},{3,1},{4,6},{5,7},{6,4},{7,5},{8,10},{9,11},{10,... | collective-permute-start | bytes 4718600 | tf_op jit(solution)/shard_map/ppermute | solution.py:188
  20.6 1.7 slice_reduce_fusion
  22.3 3.5 %collective-permute-start.21 = (f32[1024]{0:T(1024)S(1)}, f32[1024]{0:T(1024)S(1)}, u32[]{:S(2)}, u32[]{:S(2)}) collective-permute-start(f32[1024]{0:T(1024)S(1)} %get-tuple-element.14), channel_id=1, source_target_pairs={{0,8},{8,16},{16,24},{1,9},{9,17},{17,25},{2,10},{10,18},{18,26},{... | collective-permute-start | bytes 12296 | tf_op jit(solution)/shard_map/ppermute | solution.py:44
  25.8 1.3 collective-permute-start.20
  27.1 1.6 collective-permute-start.10
  28.7 2.6 %collective-permute-done.20 = f32[1024]{0:T(1024)S(1)} collective-permute-done((f32[1024]{0:T(1024)S(1)}, f32[1024]{0:T(1024)S(1)}, u32[]{:S(2)}, u32[]{:S(2)}) %collective-permute-start.20) | collective-permute-done | bytes 4128 | tf_op jit(solution)/shard_map/ppermute | solution.py:45
  31.8 24.0 %collective-permute-done.7.refs_0_ = f32[512,768]{1,0:T(8,128)S(1)} collective-permute-done((f32[512,768]{1,0:T(8,128)}, f32[512,768]{1,0:T(8,128)S(1)}, u32[]{:S(2)}, u32[]{:S(2)}) %collective-permute-start.7) | collective-permute-done | bytes 1572896 | tf_op jit(solution)/shard_map/ppermute | solution.py:188
  55.8 2.0 %collective-permute-start.15 = (f32[512,768]{1,0:T(8,128)}, f32[512,768]{1,0:T(8,128)}, u32[]{:S(2)}, u32[]{:S(2)}) collective-permute-start(f32[512,768]{1,0:T(8,128)} %get-tuple-element.22), channel_id=1, source_target_pairs={{0,4},{1,5},{2,6},{3,7},{4,0},{5,1},{6,2},{7,3},{8,12},{9,13},{10,... | collective-permute-start | bytes 4718600 | tf_op jit(solution)/shard_map/ppermute | solution.py:188
  57.9 13.7 %partial_jumps.2 = (f32[4,1024,256]{2,1,0:T(8,128)}, f32[8,1024]{1,0:T(8,128)}) custom-call(s32[1]{0:T(128)} %bitcast.at, f32[1024,1024]{1,0:T(8,128)} %refs_0_.1, f32[8192,1024]{1,0:T(8,128)} %refs_7_.5), custom_call_target="tpu_custom_call" | custom-call | flops 6442450944 | bytes 25165824 | tf_op jit(solution)/shard_map/partial_jumps/pallas_call | solution.py:138
  72.9 16.5 %collective-permute-done.13.refs_0_ = f32[512,768]{1,0:T(8,128)} collective-permute-done((f32[512,768]{1,0:T(8,128)}, f32[512,768]{1,0:T(8,128)}, u32[]{:S(2)}, u32[]{:S(2)}) %collective-permute-start.13) | collective-permute-done | bytes 1572896 | tf_op jit(solution)/shard_map/ppermute | solution.py:188
  89.4 1.7 collective-permute-start.11
  91.2 6.3 %collective-permute-done.15.refs_2_ = f32[512,768]{1,0:T(8,128)} collective-permute-done((f32[512,768]{1,0:T(8,128)}, f32[512,768]{1,0:T(8,128)}, u32[]{:S(2)}, u32[]{:S(2)}) %collective-permute-start.15) | collective-permute-done | bytes 1572896 | tf_op jit(solution)/shard_map/ppermute | solution.py:188
  97.5 1.6 collective-permute-start.8
  99.1 11.7 %fusion.4.refs_4_ = f32[1024,1024]{1,0:T(8,128)} fusion(f32[1024,1024]{1,0:T(8,128)} %refs_0_.1, f32[1024,1]{1,0:T(8,128)S(1)} %copy.9, f32[1024,1]{1,0:T(8,128)S(1)} %copy.10, f32[1024]{0:T(1024)S(1)} %get-tuple-element.26, f32[1024]{0:T(1024)S(1)} %get-tuple-element.23, f32[1024]{0:T(1024)S(1)} %get-tuple-element.24, f32[1024]{0:T(1024)S(1)} %get-tuple-element.25, ...), kind=kLoop, calls=%fused_computation.5 | loop fusion | flops 33554432 | bytes 8417280 | tf_op jit(solution)/shard_map/add | solution.py:53
  110.7 2.8 %fusion.8 = (f32[512,256]{1,0:T(8,128)}, f32[512,256]{1,0:T(8,128)}, f32[512,256]{1,0:T(8,128)S(1)}, f32[512,256]{1,0:T(8,128)}) fusion(f32[4,1024,256]{2,1,0:T(8,128)} %collective-permute-done, f32[4,1024,256]{2,1,0:T(8,128)S(1)} %copy-done), kind=kLoop, calls=%fused_computation.14 | loop fusion | flops 524288 | bytes 6291456 | tf_op jit(solution)/shard_map/add | solution.py:218
  113.6 1.2 copy-done.3
  115.2 16.5 %add_jumps.4.refs_8_ = f32[1024,1024]{1,0:T(8,128)} custom-call(s32[1]{0:T(128)} %bitcast.at, f32[1024,1024]{1,0:T(8,128)} %refs_0_.1, f32[1024,1024]{1,0:T(8,128)} %collective-permute-done.19.refs_1_, f32[8192,1024]{1,0:T(8,128)} %refs_7_.5, f32[8192,1024]{1,0:T(8,128)} %refs_7_.5, f32[1024,1024]{1,0:T(8,128)} %fusion.4.refs_4_), custom_call_target="tpu_custom_call", output_to_operand_aliasing={{}: (5, {})} | custom-call | flops 9663676416 | bytes 20971520 | tf_op jit(solution)/shard_map/add_jumps/pallas_call | solution.py:100
  131.9 2.4 %collective-permute-done.8.refs_0_ = f32[512,768]{1,0:T(8,128)} collective-permute-done((f32[512,768]{1,0:T(8,128)S(1)}, f32[512,768]{1,0:T(8,128)}, u32[]{:S(2)}, u32[]{:S(2)}) %collective-permute-start.8) | collective-permute-done | bytes 1572896 | tf_op jit(solution)/shard_map/ppermute | solution.py:188
  135.0 16.6 %add_jumps.5.refs_8_ = f32[1024,1024]{1,0:T(8,128)} custom-call(s32[1]{0:T(128)} %bitcast.at, f32[512,768]{1,0:T(8,128)} %copy-done.1, f32[512,768]{1,0:T(8,128)} %copy-done.3, f32[512,768]{1,0:T(8,128)} %collective-permute-done.10.refs_2_, f32[512,768]{1,0:T(8,128)} %collective-permute-done.18.refs_3_, ...), custom_call_target="tpu_custom_call", output_to_operand_aliasing={{}: (9, {})} | custom-call | flops 9663676416 | bytes 20971520 | tf_op jit(solution)/shard_map/add_jumps/pallas_call | solution.py:100
  151.6 1.6 collective-permute-start.5
  153.2 1.5 collective-permute-start.1
  154.7 16.6 %add_jumps.6.refs_8_ = f32[1024,1024]{1,0:T(8,128)} custom-call(s32[1]{0:T(128)} %bitcast.at, f32[512,768]{1,0:T(8,128)} %collective-permute-done.13.refs_0_, f32[512,768]{1,0:T(8,128)} %collective-permute-done.14.refs_1_, f32[512,768]{1,0:T(8,128)} %collective-permute-done.15.refs_2_, ...), custom_call_target="tpu_custom_call", output_to_operand_aliasing={{}: (9, {})} | custom-call | flops 9663676416 | bytes 20971520 | tf_op jit(solution)/shard_map/add_jumps/pallas_call | solution.py:100
  171.3 2.7 %fusion.7.own_part = f32[1024,256]{1,0:T(8,128)} fusion(f32[4,1024,256]{2,1,0:T(8,128)} %collective-permute-done, f32[4,1024,256]{2,1,0:T(8,128)} %get-tuple-element.9), kind=kLoop, calls=%fused_computation.12 | loop fusion | flops 262144 | bytes 3145728 | tf_op jit(solution)/shard_map/add | solution.py:233
  174.5 3.0 %fusion.10 = (f32[512,256]{1,0:T(8,128)}, f32[512,256]{1,0:T(8,128)}) fusion(f32[512,256]{1,0:T(8,128)} %collective-permute-done.5, f32[4,1024,256]{2,1,0:T(8,128)} %collective-permute-done, f32[4,1024,256]{2,1,0:T(8,128)} %get-tuple-element.9, f32[512,256]{1,0:T(8,128)} %collective-permute-done.3), kind=kLoop, calls=%fused_computation.17 | loop fusion | flops 524288 | bytes 4194304 | tf_op jit(solution)/shard_map/add | solution.py:224
  177.5 1.5 collective-permute-start.4
  179.6 1.2 copy-done.2
  180.7 16.6 %add_jumps.7.old = f32[1024,1024]{1,0:T(8,128)} custom-call(s32[1]{0:T(128)} %bitcast.at, f32[512,768]{1,0:T(8,128)} %collective-permute-done.8.refs_0_, f32[512,768]{1,0:T(8,128)} %copy-done.2, f32[512,768]{1,0:T(8,128)} %collective-permute-done.11.refs_2_, f32[512,768]{1,0:T(8,128)} %collective-permute-done.12.refs_3_, ...), custom_call_target="tpu_custom_call", output_to_operand_aliasing={{}: (9, {})} | custom-call | flops 9663676416 | bytes 20971520 | tf_op jit(solution)/shard_map/add_jumps/pallas_call | solution.py:100
  197.4 1.3 collective-permute-done.4.combined_a
  198.7 0.8 copy-done.6
  199.5 3.3 %add_last.1 = f32[1024,1024]{1,0:T(8,128)} custom-call(f32[512,256]{1,0:T(8,128)} %collective-permute-done.1.plain_a, f32[512,256]{1,0:T(8,128)} %collective-permute-done.2.plain_b, f32[512,256]{1,0:T(8,128)} %copy-done.6, f32[512,256]{1,0:T(8,128)} %collective-permute-done.6.combined_b, ...), custom_call_target="tpu_custom_call", output_to_operand_aliasing={{}: (5, {})} | custom-call | tf_op jit(solution)/shard_map/add_last/pallas_call | solution.py:175
  (50 shorter events, 5.0 us)
Async XLA Ops:
  13.6 83.8 %collective-permute-start = (f32[4,1024,256]{2,1,0:T(8,128)}, f32[4,1024,256]{2,1,0:T(8,128)}, u32[]{:S(2)}, u32[]{:S(2)}) collective-permute-start(f32[4,1024,256]{2,1,0:T(8,128)} %get-tuple-element.10), channel_id=1, source_target_pairs={{0,1},{1,0},{2,3},{3,2},{4,5},{5,4},{6,7},{7,6},{8,9},{9,8},{10,11... | collective-permute-start | bytes 12582920 | tf_op jit(solution)/shard_map/ppermute | solution.py:188
  17.9 37.9 %collective-permute-start.7 = (f32[512,768]{1,0:T(8,128)}, f32[512,768]{1,0:T(8,128)S(1)}, u32[]{:S(2)}, u32[]{:S(2)}) collective-permute-start(f32[512,768]{1,0:T(8,128)} %get-tuple-element.22), channel_id=1, source_target_pairs={{0,2},{1,3},{2,0},{3,1},{4,6},{5,7},{6,4},{7,5},{8,10},{9,11},{10,... | collective-permute-start | bytes 4718600 | tf_op jit(solution)/shard_map/ppermute | solution.py:188
  20.3 94.5 %collective-permute-start.19 = (f32[1024,1024]{1,0:T(8,128)}, f32[1024,1024]{1,0:T(8,128)}, u32[]{:S(2)}, u32[]{:S(2)}) collective-permute-start(f32[1024,1024]{1,0:T(8,128)} %refs_0_.1), channel_id=1, source_target_pairs={{0,1},{1,0},{2,3},{3,2},{4,5},{5,4},{6,7},{7,6},{8,9},{9,8},{10,11... | collective-permute-start | bytes 12582920 | tf_op jit(solution)/shard_map/ppermute | solution.py:188
  22.3 4.8 %collective-permute-start.21 = (f32[1024]{0:T(1024)S(1)}, f32[1024]{0:T(1024)S(1)}, u32[]{:S(2)}, u32[]{:S(2)}) collective-permute-start(f32[1024]{0:T(1024)S(1)} %get-tuple-element.14), channel_id=1, source_target_pairs={{0,8},{8,16},{16,24},{1,9},{9,17},{17,25},{2,10},{10,18},{18,26},{... | collective-permute-start | bytes 12296 | tf_op jit(solution)/shard_map/ppermute | solution.py:44
  25.8 5.5 %collective-permute-start.20 = (f32[1024]{0:T(1024)S(1)}, f32[1024]{0:T(1024)S(1)}, u32[]{:S(2)}, u32[]{:S(2)}) collective-permute-start(f32[1024]{0:T(1024)S(1)} %get-tuple-element.13), channel_id=1, source_target_pairs={{8,0},{16,8},{24,16},{9,1},{17,9},{25,17},{10,2},{18,10},{26,18},{... | collective-permute-start | bytes 12296 | tf_op jit(solution)/shard_map/ppermute | solution.py:45
  27.1 45.8 %collective-permute-start.10 = (f32[512,768]{1,0:T(8,128)}, f32[512,768]{1,0:T(8,128)}, u32[]{:S(2)}, u32[]{:S(2)}) collective-permute-start(f32[512,768]{1,0:T(8,128)} %get-tuple-element.21), channel_id=1, source_target_pairs={{0,4},{1,5},{2,6},{3,7},{4,0},{5,1},{6,2},{7,3},{8,12},{9,13},{10,... | collective-permute-start | bytes 4718600 | tf_op jit(solution)/shard_map/ppermute | solution.py:188
  31.3 58.2 %collective-permute-start.13 = (f32[512,768]{1,0:T(8,128)}, f32[512,768]{1,0:T(8,128)}, u32[]{:S(2)}, u32[]{:S(2)}) collective-permute-start(f32[512,768]{1,0:T(8,128)} %get-tuple-element.21), channel_id=1, source_target_pairs={{0,2},{1,3},{2,0},{3,1},{4,6},{5,7},{6,4},{7,5},{8,10},{9,11},{10,... | collective-permute-start | bytes 4718600 | tf_op jit(solution)/shard_map/ppermute | solution.py:188
  55.8 41.7 %copy-start.1 = (f32[512,768]{1,0:T(8,128)}, f32[512,768]{1,0:T(8,128)S(1)}, u32[]{:S(2)}) copy-start(f32[512,768]{1,0:T(8,128)S(1)} %collective-permute-done.7.refs_0_) | copy-start | bytes 4718596
  55.8 41.7 %collective-permute-start.15 = (f32[512,768]{1,0:T(8,128)}, f32[512,768]{1,0:T(8,128)}, u32[]{:S(2)}, u32[]{:S(2)}) collective-permute-start(f32[512,768]{1,0:T(8,128)} %get-tuple-element.22), channel_id=1, source_target_pairs={{0,4},{1,5},{2,6},{3,7},{4,0},{5,1},{6,2},{7,3},{8,12},{9,13},{10,... | collective-permute-start | bytes 4718600 | tf_op jit(solution)/shard_map/ppermute | solution.py:188
  57.8 13.7 %copy-start.7 = (f32[8,1024]{1,0:T(8,128)S(1)}, f32[8,1024]{1,0:T(8,128)}, u32[]{:S(2)}) copy-start(f32[8,1024]{1,0:T(8,128)} %get-tuple-element.11) | copy-start | bytes 98308
  57.8 14.5 %copy-start.8 = (f32[1024]{0:T(1024)S(1)}, f32[1024]{0:T(1024)}, u32[]{:S(2)}) copy-start(f32[1024]{0:T(1024)} %param.4) | copy-start | bytes 12292
  72.9 61.5 %collective-permute-start.18 = (f32[512,768]{1,0:T(8,128)}, f32[512,768]{1,0:T(8,128)}, u32[]{:S(2)}, u32[]{:S(2)}) collective-permute-start(f32[512,768]{1,0:T(8,128)} %collective-permute-done.10.refs_2_), channel_id=1, source_target_pairs={{0,1},{1,0},{2,3},{3,2},{4,5},{5,4},{6,7},{7,6},{8,9},{9,8},{10,11... | collective-permute-start | bytes 4718600 | tf_op jit(solution)/shard_map/ppermute | solution.py:188
  89.4 42.4 %collective-permute-start.11 = (f32[512,768]{1,0:T(8,128)}, f32[512,768]{1,0:T(8,128)}, u32[]{:S(2)}, u32[]{:S(2)}) collective-permute-start(f32[512,768]{1,0:T(8,128)} %collective-permute-done.10.refs_2_), channel_id=1, source_target_pairs={{0,2},{1,3},{2,0},{3,1},{4,6},{5,7},{6,4},{7,5},{8,10},{9,11},{10,... | collective-permute-start | bytes 4718600 | tf_op jit(solution)/shard_map/ppermute | solution.py:188
  97.5 16.1 %collective-permute-start.17 = (f32[512,768]{1,0:T(8,128)S(1)}, f32[512,768]{1,0:T(8,128)S(1)}, u32[]{:S(2)}, u32[]{:S(2)}) collective-permute-start(f32[512,768]{1,0:T(8,128)S(1)} %collective-permute-done.7.refs_0_), channel_id=1, source_target_pairs={{0,1},{1,0},{2,3},{3,2},{4,5},{5,4},{6,7},{7,6},{8,9},{9,8},{10,11... | collective-permute-start | bytes 4718600 | tf_op jit(solution)/shard_map/ppermute | solution.py:188
  97.5 36.9 %collective-permute-start.8 = (f32[512,768]{1,0:T(8,128)S(1)}, f32[512,768]{1,0:T(8,128)}, u32[]{:S(2)}, u32[]{:S(2)}) collective-permute-start(f32[512,768]{1,0:T(8,128)S(1)} %collective-permute-done.7.refs_0_), channel_id=1, source_target_pairs={{0,4},{1,5},{2,6},{3,7},{4,0},{5,1},{6,2},{7,3},{8,12},{9,13},{10,... | collective-permute-start | bytes 4718600 | tf_op jit(solution)/shard_map/ppermute | solution.py:188
  99.1 11.7 %copy-start = (f32[4,1024,256]{2,1,0:T(8,128)S(1)}, f32[4,1024,256]{2,1,0:T(8,128)}, u32[]{:S(2)}) copy-start(f32[4,1024,256]{2,1,0:T(8,128)} %get-tuple-element.9) | copy-start | bytes 12582916
  113.6 1.2 copy-start.3
  114.7 36.9 %collective-permute-start.14 = (f32[512,768]{1,0:T(8,128)}, f32[512,768]{1,0:T(8,128)}, u32[]{:S(2)}, u32[]{:S(2)}) collective-permute-start(f32[512,768]{1,0:T(8,128)} %collective-permute-done.13.refs_0_), channel_id=1, source_target_pairs={{0,1},{1,0},{2,3},{3,2},{4,5},{5,4},{6,7},{7,6},{8,9},{9,8},{10,11... | collective-permute-start | bytes 4718600 | tf_op jit(solution)/shard_map/ppermute | solution.py:188
  114.9 38.3 %collective-permute-start.16 = (f32[512,768]{1,0:T(8,128)}, f32[512,768]{1,0:T(8,128)}, u32[]{:S(2)}, u32[]{:S(2)}) collective-permute-start(f32[512,768]{1,0:T(8,128)} %collective-permute-done.15.refs_2_), channel_id=1, source_target_pairs={{0,1},{1,0},{2,3},{3,2},{4,5},{5,4},{6,7},{7,6},{8,9},{9,8},{10,11... | collective-permute-start | bytes 4718600 | tf_op jit(solution)/shard_map/ppermute | solution.py:188
  131.8 47.3 %collective-permute-start.12 = (f32[512,768]{1,0:T(8,128)}, f32[512,768]{1,0:T(8,128)}, u32[]{:S(2)}, u32[]{:S(2)}) collective-permute-start(f32[512,768]{1,0:T(8,128)} %collective-permute-done.11.refs_2_), channel_id=1, source_target_pairs={{0,1},{1,0},{2,3},{3,2},{4,5},{5,4},{6,7},{7,6},{8,9},{9,8},{10,11... | collective-permute-start | bytes 4718600 | tf_op jit(solution)/shard_map/ppermute | solution.py:188
  134.4 45.2 %collective-permute-start.9 = (f32[512,768]{1,0:T(8,128)}, f32[512,768]{1,0:T(8,128)S(1)}, u32[]{:S(2)}, u32[]{:S(2)}) collective-permute-start(f32[512,768]{1,0:T(8,128)} %collective-permute-done.8.refs_0_), channel_id=1, source_target_pairs={{0,1},{1,0},{2,3},{3,2},{4,5},{5,4},{6,7},{7,6},{8,9},{9,8},{10,11... | collective-permute-start | bytes 4718600 | tf_op jit(solution)/shard_map/ppermute | solution.py:188
  134.4 17.2 %copy-start.5 = (f32[512,256]{1,0:T(8,128)S(1)}, f32[512,256]{1,0:T(8,128)}, u32[]{:S(2)}) copy-start(f32[512,256]{1,0:T(8,128)} %get-tuple-element.17) | copy-start | bytes 1572868
  134.4 18.8 %copy-start.4 = (f32[512,256]{1,0:T(8,128)S(1)}, f32[512,256]{1,0:T(8,128)}, u32[]{:S(2)}) copy-start(f32[512,256]{1,0:T(8,128)} %get-tuple-element.20) | copy-start | bytes 1572868
  134.4 39.6 %collective-permute-start.3 = (f32[512,256]{1,0:T(8,128)}, f32[512,256]{1,0:T(8,128)}, u32[]{:S(2)}, u32[]{:S(2)}) collective-permute-start(f32[512,256]{1,0:T(8,128)} %get-tuple-element.18), channel_id=1, source_target_pairs={{0,2},{1,3},{2,0},{3,1},{4,6},{5,7},{6,4},{7,5},{8,10},{9,11},{10,... | collective-permute-start | bytes 1572872 | tf_op jit(solution)/shard_map/ppermute | solution.py:188
  151.6 22.9 %collective-permute-start.5 = (f32[512,256]{1,0:T(8,128)S(1)}, f32[512,256]{1,0:T(8,128)}, u32[]{:S(2)}, u32[]{:S(2)}) collective-permute-start(f32[512,256]{1,0:T(8,128)S(1)} %copy-done.5), channel_id=1, source_target_pairs={{0,4},{1,5},{2,6},{3,7},{4,0},{5,1},{6,2},{7,3},{8,12},{9,13},{10,... | collective-permute-start | bytes 1572872 | tf_op jit(solution)/shard_map/ppermute | solution.py:188
  153.2 44.1 %collective-permute-start.1 = (f32[512,256]{1,0:T(8,128)S(1)}, f32[512,256]{1,0:T(8,128)}, u32[]{:S(2)}, u32[]{:S(2)}) collective-permute-start(f32[512,256]{1,0:T(8,128)S(1)} %copy-done.4), channel_id=1, source_target_pairs={{0,2},{1,3},{2,0},{3,1},{4,6},{5,7},{6,4},{7,5},{8,10},{9,11},{10,... | collective-permute-start | bytes 1572872 | tf_op jit(solution)/shard_map/ppermute | solution.py:188
  174.0 23.4 %collective-permute-start.2 = (f32[512,256]{1,0:T(8,128)S(1)}, f32[512,256]{1,0:T(8,128)}, u32[]{:S(2)}, u32[]{:S(2)}) collective-permute-start(f32[512,256]{1,0:T(8,128)S(1)} %get-tuple-element.19), channel_id=1, source_target_pairs={{0,4},{1,5},{2,6},{3,7},{4,0},{5,1},{6,2},{7,3},{8,12},{9,13},{10,... | collective-permute-start | bytes 1572872 | tf_op jit(solution)/shard_map/ppermute | solution.py:188
  177.5 21.1 %collective-permute-start.4 = (f32[512,256]{1,0:T(8,128)}, f32[512,256]{1,0:T(8,128)S(1)}, u32[]{:S(2)}, u32[]{:S(2)}) collective-permute-start(f32[512,256]{1,0:T(8,128)} %get-tuple-element.16), channel_id=1, source_target_pairs={{0,4},{1,5},{2,6},{3,7},{4,0},{5,1},{6,2},{7,3},{8,12},{9,13},{10,... | collective-permute-start | bytes 1572872 | tf_op jit(solution)/shard_map/ppermute | solution.py:188
  179.1 19.6 %collective-permute-start.6 = (f32[512,256]{1,0:T(8,128)}, f32[512,256]{1,0:T(8,128)}, u32[]{:S(2)}, u32[]{:S(2)}) collective-permute-start(f32[512,256]{1,0:T(8,128)} %get-tuple-element.15), channel_id=1, source_target_pairs={{0,2},{1,3},{2,0},{3,1},{4,6},{5,7},{6,4},{7,5},{8,10},{9,11},{10,... | collective-permute-start | bytes 1572872 | tf_op jit(solution)/shard_map/ppermute | solution.py:188
  179.6 1.2 copy-start.2
  198.7 0.8 copy-start.6

commit v2 on v1

--- a/solution.py
+++ b/solution.py
@@ -5,6 +5,8 @@
 from jax.experimental.pallas import tpu as pltpu
 from jax.sharding import PartitionSpec as P
 
+
+ADD_VMEM, PART_VMEM = 28, 28
 
 interest = 0.03
 premium = 0.3
@@ -66,15 +68,16 @@
     return lax.dot_general(a, b, (((0,), (0,)), ((), ())), preferred_element_type=jnp.float32)
 
 
-def add_jumps(total, rates, me, pieces, cols, tile=256):
+def add_jumps(total, rates, me, pieces, cols, parts=(), tile=256):
     rows, width = total.shape
+    span = width if parts else cols
     count = len(pieces)
     values = [p for p, _, _ in pieces]
     depth = sum(p.shape[0] for p in values)
 
     def body(at, *refs):
         value, rate = refs[:count], refs[count : 2 * count]
-        old, new, high, low = refs[2 * count :]
+        extra, (old, new, high, low) = refs[2 * count : -4], refs[-4:]
 
         @pl.when(pl.program_id(0) == 0)
         def _():
@@ -86,7 +89,9 @@
 
         rate_high, rate_low = split(jnp.concatenate([ref[...] for ref in rate], axis=0))
         acc = dot_rows(rate_low, high[...]) + dot_rows(rate_high, low[...])
-        new[...] = old[...] + time_step * (dot_rows(rate_high, high[...]) + acc)
+        new[:, :cols] = old[:, :cols] + time_step * (dot_rows(rate_high, high[...]) + acc)
+        if parts:
+            new[:, cols:] = old[:, cols:] + time_step * sum(ref[0] for ref in extra)
 
     def rate_block(p, bits, first):
         size = p.shape[0]
@@ -94,9 +99,13 @@
             (size, tile), lambda m, at: ((at[0] ^ bits) * (rows // size) + first // size, m)
         )
 
-    specs = [pl.BlockSpec((p.shape[0], cols), lambda m, at: (0, 0)) for p in values]
+    specs = [
+        pl.BlockSpec((p.shape[0], cols), lambda m, at: (0, 0), pipeline_mode=pl.Buffered(1))
+        for p in values
+    ]
     specs += [rate_block(*piece) for piece in pieces]
-    specs += [pl.BlockSpec((tile, cols), lambda m, at: (m, 0))]
+    specs += [pl.BlockSpec((1, tile, width - cols), lambda m, at: (0, m, 0)) for _ in parts]
+    specs += [pl.BlockSpec((tile, span), lambda m, at: (m, 0))]
     return pl.pallas_call(
         body,
         out_shape=jax.ShapeDtypeStruct((rows, width), jnp.float32),
@@ -104,20 +113,21 @@
             num_scalar_prefetch=1,
             grid=(rows // tile,),
             in_specs=specs,
-            out_specs=pl.BlockSpec((tile, cols), lambda m, at: (m, 0)),
+            out_specs=pl.BlockSpec((tile, span), lambda m, at: (m, 0)),
             scratch_shapes=[pltpu.VMEM((depth, cols), jnp.bfloat16)] * 2,
         ),
-        input_output_aliases={1 + 2 * count: 0},
+        input_output_aliases={len(specs): 0},
         cost_estimate=pl.CostEstimate(
             flops=6 * rows * cols * depth,
             bytes_accessed=8 * rows * cols + 4 * depth * (rows + cols),
             transcendentals=0,
         ),
+        compiler_params=pltpu.CompilerParams(vmem_limit_bytes=ADD_VMEM << 20),
         name="add_jumps",
-    )(me.reshape(1), *values, *([rates] * count), total)
-
-
-def partial_jumps(value_field, rates, me, bit, wide, tile=512):
+    )(me.reshape(1), *values, *([rates] * count), *parts, total)
+
+
+def partial_jumps(value_field, rates, me, bit, wide, tile=1024):
     rows, cols = value_field.shape
     steps = rows // tile
 
@@ -157,30 +167,31 @@
         cost_estimate=pl.CostEstimate(
             flops=24 * rows * rows * wide, bytes_accessed=16 * rows * (rows + 2 * wide), transcendentals=0
         ),
+        compiler_params=pltpu.CompilerParams(vmem_limit_bytes=PART_VMEM << 20),
         name="partial_jumps",
     )(me.reshape(1), value_field, rates)
 
 
-def add_last(total, plain, combined, own):
+def add_last(total, before, combined):
     rows, cols = total.shape
-    half, wide = plain[0].shape
-
-    def body(plain_a, plain_b, combined_a, combined_b, own_part, old, new):
-        new[:half] = old[:half] + time_step * (own_part[:half] + plain_a[...] + combined_a[...])
-        new[half:] = old[half:] + time_step * (own_part[half:] + plain_b[...] + combined_b[...])
+    half, wide = combined[0].shape
+
+    def body(first, combined_a, combined_b, old, new):
+        new[:half] = first[:half] + time_step * combined_a[...]
+        new[half:] = first[half:] + time_step * combined_b[...]
 
     part = pl.BlockSpec((half, wide), lambda m: (0, 0))
     whole = pl.BlockSpec((rows, wide), lambda m: (0, 0))
-    last = pl.BlockSpec((rows, wide), lambda m: (0, cols // wide - 1))
     return pl.pallas_call(
         body,
         grid=(1,),
         out_shape=jax.ShapeDtypeStruct((rows, cols), jnp.float32),
-        in_specs=[part] * 4 + [whole, last],
-        out_specs=last,
-        input_output_aliases={5: 0},
+        in_specs=[whole, part, part, pl.BlockSpec(memory_space=pl.ANY)],
+        out_specs=pl.BlockSpec((rows, wide), lambda m: (0, cols // wide - 1)),
+        input_output_aliases={3: 0},
+        compiler_params=pltpu.CompilerParams(vmem_limit_bytes=16 << 20),
         name="add_last",
-    )(*plain, *combined, own, total)
+    )(before, *combined, total)
 
 
 def swap(x, bit):
@@ -198,15 +209,16 @@
     narrow = cols - wide
     me = lax.axis_index("income")
 
-    def add(total, items):
-        return add_jumps(total, jump_rates, me, items, narrow)
+    def add(total, items, parts=()):
+        return add_jumps(total, jump_rates, me, items, narrow, parts)
 
     def both(v, bits, first):
         return [(v, bits, first), (swap(v, 1), bits ^ 1, first)]
 
-    half_a, half_b = value_field[:half, :narrow], value_field[half:, :narrow]
-    x_a, y_b = swap(half_a, 2), swap(half_b, 4)
-    x_b, y_a = swap(half_b, 2), swap(half_a, 4)
+    whole, half_a = lax.optimization_barrier((value_field, value_field[:half, :narrow]))
+    half_b = whole[half:, :narrow]
+    x_a, y_a = swap(half_a, 2), swap(half_a, 4)
+    x_b, y_b = swap(half_b, 2), swap(half_b, 4)
     far_a, far_b = swap(x_a, 4), swap(y_b, 2)
     other = swap(value_field, 1)
 
@@ -226,11 +238,14 @@
 
     outflow = jnp.sum(sums_send + sums_keep, axis=0)
     total = base_part(value_field, income, outflow)
-    total = add(total, [(value_field, 0, 0), (other, 1, 0)])
-    total = add(total, both(x_a, 2, 0) + both(y_b, 4, half))
-    total = add(total, both(x_b, 2, half) + both(y_a, 4, 0))
-    total = add(total, both(far_a, 6, 0) + both(far_b, 6, half))
-    return add_last(total, (plain_x, plain_y), (comb_y, comb_x), keep[0] + got[0])
+    total = add(total, [(value_field, 0, 0), (other, 1, 0)], (keep, got))
+    total = add(total, both(x_a, 2, 0) + both(y_a, 4, 0))
+    total = add(total, both(x_b, 2, half) + both(y_b, 4, half))
+    total = add(total, both(far_a, 6, 0))
+    total = add(total, both(far_b, 6, half))
+    plain = jnp.concatenate([plain_x, plain_y], axis=0)
+    before = total[:, narrow:] + time_step * plain
+    return add_last(total, before, (comb_y, comb_x))
 
 
 def local_any(value_field, income, jump_rates):

time: 204 us -> 196 us (0.961)
  Pallas kernels: 97 us -> 88.6 us
  waiting for transfers between devices: 53.2 us -> 58.2 us
  other arithmetic: 21 us -> 16.4 us
  local copies, waits for them, and re-layouts: 9.04 us -> 11.1 us
    ppermute x20, waiting for transfers between devices: 50.6 us -> 58.2 us  [swap(): return lax.ppermute(x, 'income', [(i, i ^ bit) for i in range(count)])]
    pallas_call x2, Pallas kernels: 27.3 us -> 22.4 us  [partial_jumps(): pl.pallas_call(body, out_shape=(jax.ShapeDtypeStruct((4, rows, wide), jnp...]
    ppermute x20, starting transfers between devices: 17.7 us -> 14.7 us  [swap(): return lax.ppermute(x, 'income', [(i, i ^ bit) for i in range(count)])]
    ppermute x1, waiting for transfers between devices: 2.6 us -> 0.01 us  [base_part(): after = lax.ppermute(value_field[:, 0], 'wealth', down)]
    pallas_call x1, Pallas kernels: 3.33 us -> 1.08 us  [add_last(): pl.pallas_call(body, grid=(1,), out_shape=jax.ShapeDtypeStruct((rows, col...]
    slice x1 -> x2, local copies, waits for them, and re-layouts: 3.74 us -> 5.34 us  [the longest x1 2.68 us: step_grid(): half_b = whole[half:, :narrow]]
    pallas_call x4 -> x5, Pallas kernels: 66.3 us -> 65.1 us  [add_jumps(): pl.pallas_call(body, out_shape=jax.ShapeDtypeStruct((rows, width), jnp.fl...]
  transfers between devices with their start and end apart: 22 -> 22, of which waited for: 6 -> 5; matrix products, arithmetic and copies ran while one was open for 13% -> 13% of each run, Pallas kernels for 39% -> 39%
where the time goes in v2:
time: 196 us; the launch traced here: 195 us
  Pallas kernels  88.6 us (45%)
  waiting for transfers between devices  58.2 us (30%)
  starting transfers between devices  20.5 us (10%)
  other arithmetic  16.4 us (8%)
  local copies, waits for them, and re-layouts  11.1 us (6%)
    pallas_call x5, Pallas kernels, add_jumps(): pl.pallas_call(body, out_shape=jax.ShapeDtypeStruct((rows, width), jnp.fl...  65.1 us
    ppermute x20, waiting for transfers between devices, swap(): return lax.ppermute(x, 'income', [(i, i ^ bit) for i in range(count)])  58.2 us
    pallas_call x2, Pallas kernels, partial_jumps(): pl.pallas_call(body, out_shape=(jax.ShapeDtypeStruct((4, rows, wide), jnp...  22.4 us
    ppermute x20, starting transfers between devices, swap(): return lax.ppermute(x, 'income', [(i, i ^ bit) for i in range(count)])  14.7 us
    add x1, other arithmetic, base_part(): value_field + time_step * (local_part - (outflow[:, None] + discount) * v...  11.8 us
    ppermute x1, starting transfers between devices, base_part(): before = lax.ppermute(value_field[:, -1], 'wealth', up)  4.55 us
  transfers between devices with their start and end apart: 22, of which 5 were waited for; matrix products, arithmetic and copies ran while one was open for 13% of the time, Pallas kernels for 39%

profile of v2, /device:TPU:0, one launch (start us, length us, event | category | flops | bytes accessed | tf_op | source)
XLA Modules:
  0.0 195.0 jit_solution(4506713209489163481)
XLA Ops:
  0.0 11.8 %partial_jumps.3 = (f32[4,1024,256]{2,1,0:T(8,128)}, f32[8,1024]{1,0:T(8,128)S(1)}) custom-call(s32[1]{0:T(128)} %bitcast.at, f32[1024,1024]{1,0:T(8,128)} %refs_0_.1, f32[8192,1024]{1,0:T(8,128)} %refs_3_.5), custom_call_target="tpu_custom_call" | custom-call | flops 6442450944 | bytes 25165824 | tf_op jit(solution)/shard_map/partial_jumps/pallas_call | solution.py:148
  12.3 2.7 %slice.61 = f32[512,768]{1,0:T(8,128)} slice(f32[1024,1024]{1,0:T(8,128)} %refs_0_.1), slice={[0:512], [0:768]} | slice | bytes 3145728 | tf_op jit(solution)/shard_map/slice | solution.py:218
  15.0 2.5 %collective-permute-start.3 = (f32[512,768]{1,0:T(8,128)}, f32[512,768]{1,0:T(8,128)S(1)}, u32[]{:S(2)}, u32[]{:S(2)}) collective-permute-start(f32[512,768]{1,0:T(8,128)} %slice.61), channel_id=1, source_target_pairs={{0,2},{1,3},{2,0},{3,1},{4,6},{5,7},{6,4},{7,5},{8,10},{9,11},{10,... | collective-permute-start | bytes 4718600 | tf_op jit(solution)/shard_map/ppermute | solution.py:199
  17.7 1.7 slice_reduce_fusion
  19.4 1.3 collective-permute-start.14
  20.7 4.5 %collective-permute-start.15 = (f32[1024]{0:T(1024)S(1)}, f32[1024]{0:T(1024)S(1)}, u32[]{:S(2)}, u32[]{:S(2)}) collective-permute-start(f32[1024]{0:T(1024)S(1)} %get-tuple-element.18), channel_id=1, source_target_pairs={{0,8},{8,16},{16,24},{1,9},{9,17},{17,25},{2,10},{10,18},{18,26},{... | collective-permute-start | bytes 12296 | tf_op jit(solution)/shard_map/ppermute | solution.py:46
  25.3 2.7 %slice.62 = f32[512,768]{1,0:T(8,128)} slice(f32[1024,1024]{1,0:T(8,128)} %refs_0_.1), slice={[512:1024], [0:768]} | slice | bytes 3145728 | tf_op jit(solution)/shard_map/slice | solution.py:219
  27.9 1.5 collective-permute-start.10
  30.0 22.8 %collective-permute-done.3.refs_0_ = f32[512,768]{1,0:T(8,128)S(1)} collective-permute-done((f32[512,768]{1,0:T(8,128)}, f32[512,768]{1,0:T(8,128)S(1)}, u32[]{:S(2)}, u32[]{:S(2)}) %collective-permute-start.3) | collective-permute-done | bytes 1572896 | tf_op jit(solution)/shard_map/ppermute | solution.py:199
  52.7 1.7 collective-permute-start.6
  54.5 10.6 %partial_jumps.2 = (f32[4,1024,256]{2,1,0:T(8,128)S(1)}, f32[8,1024]{1,0:T(8,128)S(1)}) custom-call(s32[1]{0:T(128)} %bitcast.at, f32[1024,1024]{1,0:T(8,128)} %refs_0_.1, f32[8192,1024]{1,0:T(8,128)} %refs_3_.5), custom_call_target="tpu_custom_call" | custom-call | flops 6442450944 | bytes 25165824 | tf_op jit(solution)/shard_map/partial_jumps/pallas_call | solution.py:148
  65.1 2.0 %copy-done = f32[4,1024,256]{2,1,0:T(8,128)} copy-done((f32[4,1024,256]{2,1,0:T(8,128)}, f32[4,1024,256]{2,1,0:T(8,128)S(1)}, u32[]{:S(2)}) %copy-start) | copy-done | bytes 4194328
  67.1 1.0 copy.10
  68.1 1.0 copy.11
  69.2 28.7 %collective-permute-done.refs_2_ = f32[512,768]{1,0:T(8,128)S(1)} collective-permute-done((f32[512,768]{1,0:T(8,128)}, f32[512,768]{1,0:T(8,128)S(1)}, u32[]{:S(2)}, u32[]{:S(2)}) %collective-permute-start) | collective-permute-done | bytes 1572896 | tf_op jit(solution)/shard_map/ppermute | solution.py:199
  97.9 1.5 collective-permute-start.4
  99.4 0.6 collective-permute-start.1
  100.0 11.8 %fusion.4.refs_6_ = f32[1024,1024]{1,0:T(8,128)} fusion(f32[1024,1024]{1,0:T(8,128)} %refs_0_.1, f32[1024,1]{1,0:T(8,128)} %copy.10, f32[1024,1]{1,0:T(8,128)} %copy.11, f32[1024]{0:T(1024)S(1)} %get-tuple-element.28, f32[1024]{0:T(1024)S(1)} %get-tuple-element.25, f32[1024]{0:T(1024)S(1)} %get-tuple-element.26, f32[1024]{0:T(1024)S(1)} %get-tuple-element.27, ...), kind=kLoop, calls=%fused_computation.5 | loop fusion | flops 33554432 | bytes 8417280 | tf_op jit(solution)/shard_map/add | solution.py:55
  111.8 1.8 fusion.7
  114.2 16.9 %add_jumps.5.refs_8_ = f32[1024,1024]{1,0:T(8,128)} custom-call(s32[1]{0:T(128)} %bitcast.at, f32[1024,1024]{1,0:T(8,128)} %refs_0_.1, f32[1024,1024]{1,0:T(8,128)} %collective-permute-done.12.refs_1_, f32[8192,1024]{1,0:T(8,128)} %refs_3_.5, f32[8192,1024]{1,0:T(8,128)} %refs_3_.5, f32[4,1024,256]{2,1,0:T(8,128)S(1)} %copy-done.1, ...), custom_call_target="tpu_custom_call", output_to_operand_aliasing={{}: (7, {})} | custom-call | flops 9663676416 | bytes 20971520 | tf_op jit(solution)/shard_map/add_jumps/pallas_call | solution.py:109
  131.1 1.9 collective-permute-done.4.refs_0_
  133.0 3.2 %collective-permute-done.1.refs_0_ = f32[512,768]{1,0:T(8,128)S(1)} collective-permute-done((f32[512,768]{1,0:T(8,128)S(1)}, f32[512,768]{1,0:T(8,128)S(1)}, u32[]{:S(2)}, u32[]{:S(2)}) %collective-permute-start.1) | collective-permute-done | bytes 1572896 | tf_op jit(solution)/shard_map/ppermute | solution.py:199
  136.8 15.2 %add_jumps.6.refs_8_ = f32[1024,1024]{1,0:T(8,128)} custom-call(s32[1]{0:T(128)} %bitcast.at, f32[512,768]{1,0:T(8,128)S(1)} %collective-permute-done.3.refs_0_, f32[512,768]{1,0:T(8,128)S(1)} %collective-permute-done.9.refs_1_, f32[512,768]{1,0:T(8,128)} %collective-permute-done.10.refs_2_, ...), custom_call_target="tpu_custom_call", output_to_operand_aliasing={{}: (9, {})} | custom-call | flops 9663676416 | bytes 20971520 | tf_op jit(solution)/shard_map/add_jumps/pallas_call | solution.py:109
  152.0 1.5 collective-permute-start.18
  154.0 15.2 %add_jumps.7.refs_4_ = f32[1024,1024]{1,0:T(8,128)} custom-call(s32[1]{0:T(128)} %bitcast.at, f32[512,768]{1,0:T(8,128)} %collective-permute-done.6.refs_0_, f32[512,768]{1,0:T(8,128)S(1)} %collective-permute-done.7.refs_1_, f32[512,768]{1,0:T(8,128)S(1)} %collective-permute-done.refs_2_, ...), custom_call_target="tpu_custom_call", output_to_operand_aliasing={{}: (9, {})} | custom-call | flops 9663676416 | bytes 20971520 | tf_op jit(solution)/shard_map/add_jumps/pallas_call | solution.py:109
  169.2 1.5 collective-permute-start.17
  170.7 1.4 fusion.9
  173.1 8.9 %add_jumps.8.refs_4_ = f32[1024,1024]{1,0:T(8,128)} custom-call(s32[1]{0:T(128)} %bitcast.at, f32[512,768]{1,0:T(8,128)S(1)} %collective-permute-done.4.refs_0_, f32[512,768]{1,0:T(8,128)S(1)} %collective-permute-done.5.refs_1_, f32[8192,1024]{1,0:T(8,128)} %refs_3_.5, f32[8192,1024]{1,0:T(8,128)} %refs_3_.5, ...), custom_call_target="tpu_custom_call", output_to_operand_aliasing={{}: (5, {})} | custom-call | flops 4831838208 | bytes 13631488 | tf_op jit(solution)/shard_map/add_jumps/pallas_call | solution.py:109
  182.0 8.9 %add_jumps.9.old = f32[1024,1024]{1,0:T(8,128)} custom-call(s32[1]{0:T(128)} %bitcast.at, f32[512,768]{1,0:T(8,128)S(1)} %collective-permute-done.1.refs_0_, f32[512,768]{1,0:T(8,128)S(1)} %collective-permute-done.2.refs_1_, f32[8192,1024]{1,0:T(8,128)} %refs_3_.5, f32[8192,1024]{1,0:T(8,128)} %refs_3_.5, ...), custom_call_target="tpu_custom_call", output_to_operand_aliasing={{}: (5, {})} | custom-call | flops 4831838208 | bytes 13631488 | tf_op jit(solution)/shard_map/add_jumps/pallas_call | solution.py:109
  190.9 1.4 slice_add_fusion.first
  192.3 1.6 collective-permute-done.19.combined_a
  193.9 1.1 add_last.1
  (40 shorter events, 3.9 us)
Async XLA Ops:
  11.8 87.6 %collective-permute-start.13 = (f32[4,1024,256]{2,1,0:T(8,128)}, f32[4,1024,256]{2,1,0:T(8,128)}, u32[]{:S(2)}, u32[]{:S(2)}) collective-permute-start(f32[4,1024,256]{2,1,0:T(8,128)} %get-tuple-element.14), channel_id=1, source_target_pairs={{0,1},{1,0},{2,3},{3,2},{4,5},{5,4},{6,7},{7,6},{8,9},{9,8},{10,11... | collective-permute-start | bytes 12582920 | tf_op jit(solution)/shard_map/ppermute | solution.py:199
  15.0 37.8 %collective-permute-start.3 = (f32[512,768]{1,0:T(8,128)}, f32[512,768]{1,0:T(8,128)S(1)}, u32[]{:S(2)}, u32[]{:S(2)}) collective-permute-start(f32[512,768]{1,0:T(8,128)} %slice.61), channel_id=1, source_target_pairs={{0,2},{1,3},{2,0},{3,1},{4,6},{5,7},{6,4},{7,5},{8,10},{9,11},{10,... | collective-permute-start | bytes 4718600 | tf_op jit(solution)/shard_map/ppermute | solution.py:199
  17.5 96.4 %collective-permute-start.12 = (f32[1024,1024]{1,0:T(8,128)}, f32[1024,1024]{1,0:T(8,128)}, u32[]{:S(2)}, u32[]{:S(2)}) collective-permute-start(f32[1024,1024]{1,0:T(8,128)} %refs_0_.1), channel_id=1, source_target_pairs={{0,1},{1,0},{2,3},{3,2},{4,5},{5,4},{6,7},{7,6},{8,9},{9,8},{10,11... | collective-permute-start | bytes 12582920 | tf_op jit(solution)/shard_map/ppermute | solution.py:199
  19.4 8.5 %collective-permute-start.14 = (f32[1024]{0:T(1024)S(1)}, f32[1024]{0:T(1024)S(1)}, u32[]{:S(2)}, u32[]{:S(2)}) collective-permute-start(f32[1024]{0:T(1024)S(1)} %get-tuple-element.17), channel_id=1, source_target_pairs={{8,0},{16,8},{24,16},{9,1},{17,9},{25,17},{10,2},{18,10},{26,18},{... | collective-permute-start | bytes 12296 | tf_op jit(solution)/shard_map/ppermute | solution.py:47
  20.7 8.8 %collective-permute-start.15 = (f32[1024]{0:T(1024)S(1)}, f32[1024]{0:T(1024)S(1)}, u32[]{:S(2)}, u32[]{:S(2)}) collective-permute-start(f32[1024]{0:T(1024)S(1)} %get-tuple-element.18), channel_id=1, source_target_pairs={{0,8},{8,16},{16,24},{1,9},{9,17},{17,25},{2,10},{10,18},{18,26},{... | collective-permute-start | bytes 12296 | tf_op jit(solution)/shard_map/ppermute | solution.py:46
  27.9 41.2 %collective-permute-start.10 = (f32[512,768]{1,0:T(8,128)}, f32[512,768]{1,0:T(8,128)}, u32[]{:S(2)}, u32[]{:S(2)}) collective-permute-start(f32[512,768]{1,0:T(8,128)} %slice.61), channel_id=1, source_target_pairs={{0,4},{1,5},{2,6},{3,7},{4,0},{5,1},{6,2},{7,3},{8,12},{9,13},{10,... | collective-permute-start | bytes 4718600 | tf_op jit(solution)/shard_map/ppermute | solution.py:199
  29.5 68.4 %collective-permute-start = (f32[512,768]{1,0:T(8,128)}, f32[512,768]{1,0:T(8,128)S(1)}, u32[]{:S(2)}, u32[]{:S(2)}) collective-permute-start(f32[512,768]{1,0:T(8,128)} %slice.62), channel_id=1, source_target_pairs={{0,4},{1,5},{2,6},{3,7},{4,0},{5,1},{6,2},{7,3},{8,12},{9,13},{10,... | collective-permute-start | bytes 4718600 | tf_op jit(solution)/shard_map/ppermute | solution.py:199
  52.7 46.7 %collective-permute-start.6 = (f32[512,768]{1,0:T(8,128)}, f32[512,768]{1,0:T(8,128)}, u32[]{:S(2)}, u32[]{:S(2)}) collective-permute-start(f32[512,768]{1,0:T(8,128)} %slice.62), channel_id=1, source_target_pairs={{0,2},{1,3},{2,0},{3,1},{4,6},{5,7},{6,4},{7,5},{8,10},{9,11},{10,... | collective-permute-start | bytes 4718600 | tf_op jit(solution)/shard_map/ppermute | solution.py:199
  54.5 13.6 %copy-start.2 = (f32[1024]{0:T(1024)S(1)}, f32[1024]{0:T(1024)}, u32[]{:S(2)}) copy-start(f32[1024]{0:T(1024)} %param.4) | copy-start | bytes 12292
  65.1 2.0 %copy-start = (f32[4,1024,256]{2,1,0:T(8,128)}, f32[4,1024,256]{2,1,0:T(8,128)S(1)}, u32[]{:S(2)}) copy-start(f32[4,1024,256]{2,1,0:T(8,128)S(1)} %get-tuple-element.13.refs_4_) | copy-start | bytes 12582916
  69.2 44.5 %collective-permute-start.9 = (f32[512,768]{1,0:T(8,128)S(1)}, f32[512,768]{1,0:T(8,128)S(1)}, u32[]{:S(2)}, u32[]{:S(2)}) collective-permute-start(f32[512,768]{1,0:T(8,128)S(1)} %collective-permute-done.3.refs_0_), channel_id=1, source_target_pairs={{0,1},{1,0},{2,3},{3,2},{4,5},{5,4},{6,7},{7,6},{8,9},{9,8},{10,11... | collective-permute-start | bytes 4718600 | tf_op jit(solution)/shard_map/ppermute | solution.py:199
  97.9 35.2 %collective-permute-start.4 = (f32[512,768]{1,0:T(8,128)S(1)}, f32[512,768]{1,0:T(8,128)S(1)}, u32[]{:S(2)}, u32[]{:S(2)}) collective-permute-start(f32[512,768]{1,0:T(8,128)S(1)} %collective-permute-done.3.refs_0_), channel_id=1, source_target_pairs={{0,4},{1,5},{2,6},{3,7},{4,0},{5,1},{6,2},{7,3},{8,12},{9,13},{10,... | collective-permute-start | bytes 4718600 | tf_op jit(solution)/shard_map/ppermute | solution.py:199
  99.4 36.8 %collective-permute-start.11 = (f32[512,768]{1,0:T(8,128)}, f32[512,768]{1,0:T(8,128)S(1)}, u32[]{:S(2)}, u32[]{:S(2)}) collective-permute-start(f32[512,768]{1,0:T(8,128)} %collective-permute-done.10.refs_2_), channel_id=1, source_target_pairs={{0,1},{1,0},{2,3},{3,2},{4,5},{5,4},{6,7},{7,6},{8,9},{9,8},{10,11... | collective-permute-start | bytes 4718600 | tf_op jit(solution)/shard_map/ppermute | solution.py:199
  99.4 36.8 %collective-permute-start.1 = (f32[512,768]{1,0:T(8,128)S(1)}, f32[512,768]{1,0:T(8,128)S(1)}, u32[]{:S(2)}, u32[]{:S(2)}) collective-permute-start(f32[512,768]{1,0:T(8,128)S(1)} %collective-permute-done.refs_2_), channel_id=1, source_target_pairs={{0,2},{1,3},{2,0},{3,1},{4,6},{5,7},{6,4},{7,5},{8,10},{9,11},{10,... | collective-permute-start | bytes 4718600 | tf_op jit(solution)/shard_map/ppermute | solution.py:199
  100.0 11.8 %copy-start.1 = (f32[4,1024,256]{2,1,0:T(8,128)S(1)}, f32[4,1024,256]{2,1,0:T(8,128)}, u32[]{:S(2)}) copy-start(f32[4,1024,256]{2,1,0:T(8,128)} %copy-done) | copy-start | bytes 12582916
  113.6 38.3 %collective-permute-start.8 = (f32[512,768]{1,0:T(8,128)S(1)}, f32[512,768]{1,0:T(8,128)S(1)}, u32[]{:S(2)}, u32[]{:S(2)}) collective-permute-start(f32[512,768]{1,0:T(8,128)S(1)} %collective-permute-done.refs_2_), channel_id=1, source_target_pairs={{0,1},{1,0},{2,3},{3,2},{4,5},{5,4},{6,7},{7,6},{8,9},{9,8},{10,11... | collective-permute-start | bytes 4718600 | tf_op jit(solution)/shard_map/ppermute | solution.py:199
  113.9 39.6 %collective-permute-start.7 = (f32[512,768]{1,0:T(8,128)}, f32[512,768]{1,0:T(8,128)S(1)}, u32[]{:S(2)}, u32[]{:S(2)}) collective-permute-start(f32[512,768]{1,0:T(8,128)} %collective-permute-done.6.refs_0_), channel_id=1, source_target_pairs={{0,1},{1,0},{2,3},{3,2},{4,5},{5,4},{6,7},{7,6},{8,9},{9,8},{10,11... | collective-permute-start | bytes 4718600 | tf_op jit(solution)/shard_map/ppermute | solution.py:199
  133.0 39.6 %collective-permute-start.5 = (f32[512,768]{1,0:T(8,128)S(1)}, f32[512,768]{1,0:T(8,128)S(1)}, u32[]{:S(2)}, u32[]{:S(2)}) collective-permute-start(f32[512,768]{1,0:T(8,128)S(1)} %collective-permute-done.4.refs_0_), channel_id=1, source_target_pairs={{0,1},{1,0},{2,3},{3,2},{4,5},{5,4},{6,7},{7,6},{8,9},{9,8},{10,11... | collective-permute-start | bytes 4718600 | tf_op jit(solution)/shard_map/ppermute | solution.py:199
  136.2 45.8 %collective-permute-start.2 = (f32[512,768]{1,0:T(8,128)S(1)}, f32[512,768]{1,0:T(8,128)S(1)}, u32[]{:S(2)}, u32[]{:S(2)}) collective-permute-start(f32[512,768]{1,0:T(8,128)S(1)} %collective-permute-done.1.refs_0_), channel_id=1, source_target_pairs={{0,1},{1,0},{2,3},{3,2},{4,5},{5,4},{6,7},{7,6},{8,9},{9,8},{10,11... | collective-permute-start | bytes 4718600 | tf_op jit(solution)/shard_map/ppermute | solution.py:199
  136.2 54.7 %collective-permute-start.16 = (f32[512,256]{1,0:T(8,128)S(1)}, f32[512,256]{1,0:T(8,128)S(1)}, u32[]{:S(2)}, u32[]{:S(2)}) collective-permute-start(f32[512,256]{1,0:T(8,128)S(1)} %get-tuple-element.24), channel_id=1, source_target_pairs={{0,2},{1,3},{2,0},{3,1},{4,6},{5,7},{6,4},{7,5},{8,10},{9,11},{10,... | collective-permute-start | bytes 1572872 | tf_op jit(solution)/shard_map/ppermute | solution.py:199
  152.0 17.2 %collective-permute-start.18 = (f32[512,256]{1,0:T(8,128)S(1)}, f32[512,256]{1,0:T(8,128)S(1)}, u32[]{:S(2)}, u32[]{:S(2)}) collective-permute-start(f32[512,256]{1,0:T(8,128)S(1)} %get-tuple-element.22), channel_id=1, source_target_pairs={{0,2},{1,3},{2,0},{3,1},{4,6},{5,7},{6,4},{7,5},{8,10},{9,11},{10,... | collective-permute-start | bytes 1572872 | tf_op jit(solution)/shard_map/ppermute | solution.py:199
  153.4 17.2 %collective-permute-start.20 = (f32[512,256]{1,0:T(8,128)S(1)}, f32[512,256]{1,0:T(8,128)S(1)}, u32[]{:S(2)}, u32[]{:S(2)}) collective-permute-start(f32[512,256]{1,0:T(8,128)S(1)} %get-tuple-element.21), channel_id=1, source_target_pairs={{0,4},{1,5},{2,6},{3,7},{4,0},{5,1},{6,2},{7,3},{8,12},{9,13},{10,... | collective-permute-start | bytes 1572872 | tf_op jit(solution)/shard_map/ppermute | solution.py:199
  169.2 21.7 %collective-permute-start.17 = (f32[512,256]{1,0:T(8,128)S(1)}, f32[512,256]{1,0:T(8,128)S(1)}, u32[]{:S(2)}, u32[]{:S(2)}) collective-permute-start(f32[512,256]{1,0:T(8,128)S(1)} %get-tuple-element.23), channel_id=1, source_target_pairs={{0,4},{1,5},{2,6},{3,7},{4,0},{5,1},{6,2},{7,3},{8,12},{9,13},{10,... | collective-permute-start | bytes 1572872 | tf_op jit(solution)/shard_map/ppermute | solution.py:199
  172.1 21.8 %collective-permute-start.19 = (f32[512,256]{1,0:T(8,128)S(1)}, f32[512,256]{1,0:T(8,128)S(1)}, u32[]{:S(2)}, u32[]{:S(2)}) collective-permute-start(f32[512,256]{1,0:T(8,128)S(1)} %get-tuple-element.20), channel_id=1, source_target_pairs={{0,4},{1,5},{2,6},{3,7},{4,0},{5,1},{6,2},{7,3},{8,12},{9,13},{10,... | collective-permute-start | bytes 1572872 | tf_op jit(solution)/shard_map/ppermute | solution.py:199
  172.7 21.3 %collective-permute-start.21 = (f32[512,256]{1,0:T(8,128)S(1)}, f32[512,256]{1,0:T(8,128)S(1)}, u32[]{:S(2)}, u32[]{:S(2)}) collective-permute-start(f32[512,256]{1,0:T(8,128)S(1)} %get-tuple-element.19), channel_id=1, source_target_pairs={{0,2},{1,3},{2,0},{3,1},{4,6},{5,7},{6,4},{7,5},{8,10},{9,11},{10,... | collective-permute-start | bytes 1572872 | tf_op jit(solution)/shard_map/ppermute | solution.py:199

commit v3 on v2

--- a/solution.py
+++ b/solution.py
@@ -194,6 +194,36 @@
     )(before, *combined, total)
 
 
+def half_rows(value_field, first, cols, chunks=8):
+    half = value_field.shape[0] // 2
+    size = half // chunks
+
+    def body(whole, part, buffer, sems):
+        loads, stores = [], []
+        for k in range(chunks):
+            span = pl.ds(k * size, size)
+            source = whole.at[pl.ds(first + k * size, size), pl.ds(0, cols)]
+            loads.append(pltpu.make_async_copy(source, buffer.at[span], sems.at[k]))
+            stores.append(pltpu.make_async_copy(buffer.at[span], part.at[span], sems.at[chunks + k]))
+        for load in loads:
+            load.start()
+        for load, store in zip(loads, stores):
+            load.wait()
+            store.start()
+        for store in stores:
+            store.wait()
+
+    return pl.pallas_call(
+        body,
+        out_shape=jax.ShapeDtypeStruct((half, cols), jnp.float32),
+        in_specs=[pl.BlockSpec(memory_space=pl.ANY)],
+        out_specs=pl.BlockSpec(memory_space=pl.ANY),
+        scratch_shapes=[pltpu.VMEM((half, cols), jnp.float32), pltpu.SemaphoreType.DMA((2 * chunks,))],
+        compiler_params=pltpu.CompilerParams(vmem_limit_bytes=8 << 20),
+        name="half_rows",
+    )(value_field)
+
+
 def swap(x, bit):
     count = lax.axis_size("income")
     return lax.ppermute(x, "income", [(i, i ^ bit) for i in range(count)])
@@ -215,8 +245,8 @@
     def both(v, bits, first):
         return [(v, bits, first), (swap(v, 1), bits ^ 1, first)]
 
-    whole, half_a = lax.optimization_barrier((value_field, value_field[:half, :narrow]))
-    half_b = whole[half:, :narrow]
+    half_a = half_rows(value_field, 0, narrow)
+    half_b = half_rows(value_field, half, narrow)
     x_a, y_a = swap(half_a, 2), swap(half_a, 4)
     x_b, y_b = swap(half_b, 2), swap(half_b, 4)
     far_a, far_b = swap(x_a, 4), swap(y_b, 2)

time: 196 us -> 195 us (level)
  local copies, waits for them, and re-layouts: 11.1 us -> 5.73 us
  Pallas kernels: 88.6 us -> 93.3 us
    slice x2 -> x0, local copies, waits for them, and re-layouts: 5.34 us -> none  [the longest x1 2.68 us: step_grid(): half_b = whole[half:, :narrow]]
    pallas_call x0 -> x2, Pallas kernels: none -> 4.61 us  [half_rows(): pl.pallas_call(body, out_shape=jax.ShapeDtypeStruct((half, cols), jnp.flo...]
  transfers between devices with their start and end apart: 22 -> 22, of which waited for: 5 -> 5; matrix products, arithmetic and copies ran while one was open for 13% -> 10% of each run, Pallas kernels for 39% -> 41%
where the time goes in v3:
time: 195 us; the launch traced here: 194 us
  Pallas kernels  93.3 us (48%)
  waiting for transfers between devices  58.2 us (30%)
  starting transfers between devices  20.7 us (11%)
  other arithmetic  16.4 us (8%)
  local copies, waits for them, and re-layouts  5.73 us (3%)
    pallas_call x5, Pallas kernels, add_jumps(): pl.pallas_call(body, out_shape=jax.ShapeDtypeStruct((rows, width), jnp.fl...  65.2 us
    ppermute x20, waiting for transfers between devices, swap(): return lax.ppermute(x, 'income', [(i, i ^ bit) for i in range(count)])  58.2 us
    pallas_call x2, Pallas kernels, partial_jumps(): pl.pallas_call(body, out_shape=(jax.ShapeDtypeStruct((4, rows, wide), jnp...  22.4 us
    ppermute x20, starting transfers between devices, swap(): return lax.ppermute(x, 'income', [(i, i ^ bit) for i in range(count)])  14.8 us
    add x1, other arithmetic, base_part(): value_field + time_step * (local_part - (outflow[:, None] + discount) * v...  11.8 us
    pallas_call x2, Pallas kernels, half_rows(): pl.pallas_call(body, out_shape=jax.ShapeDtypeStruct((half, cols), jnp.flo...  4.61 us
    ppermute x1, starting transfers between devices, base_part(): before = lax.ppermute(value_field[:, -1], 'wealth', up)  4.55 us
  transfers between devices with their start and end apart: 22, of which 5 were waited for; matrix products, arithmetic and copies ran while one was open for 10% of the time, Pallas kernels for 41%

profile of v3, /device:TPU:0, one launch (start us, length us, event | category | flops | bytes accessed | tf_op | source)
XLA Modules:
  0.0 194.4 jit_solution(1000978620585767197)
XLA Ops:
  0.0 11.8 %partial_jumps.3 = (f32[4,1024,256]{2,1,0:T(8,128)}, f32[8,1024]{1,0:T(8,128)S(1)}) custom-call(s32[1]{0:T(128)} %bitcast.at, f32[1024,1024]{1,0:T(8,128)} %refs_0_.1, f32[8192,1024]{1,0:T(8,128)} %refs_3_.5), custom_call_target="tpu_custom_call" | custom-call | flops 6442450944 | bytes 25165824 | tf_op jit(solution)/shard_map/partial_jumps/pallas_call | solution.py:148
  12.3 2.3 %half_rows.3 = f32[512,768]{1,0:T(8,128)} custom-call(f32[1024,1024]{1,0:T(8,128)} %refs_0_.1), custom_call_target="tpu_custom_call" | custom-call | tf_op jit(solution)/shard_map/half_rows/pallas_call | solution.py:216
  14.6 2.5 %collective-permute-start.3 = (f32[512,768]{1,0:T(8,128)}, f32[512,768]{1,0:T(8,128)S(1)}, u32[]{:S(2)}, u32[]{:S(2)}) collective-permute-start(f32[512,768]{1,0:T(8,128)} %half_rows.3), channel_id=1, source_target_pairs={{0,2},{1,3},{2,0},{3,1},{4,6},{5,7},{6,4},{7,5},{8,10},{9,11},{10,... | collective-permute-start | bytes 4718600 | tf_op jit(solution)/shard_map/ppermute | solution.py:229
  17.4 1.7 slice_reduce_fusion
  19.1 1.3 collective-permute-start.14
  20.4 4.5 %collective-permute-start.15 = (f32[1024]{0:T(1024)S(1)}, f32[1024]{0:T(1024)S(1)}, u32[]{:S(2)}, u32[]{:S(2)}) collective-permute-start(f32[1024]{0:T(1024)S(1)} %get-tuple-element.14), channel_id=1, source_target_pairs={{0,8},{8,16},{16,24},{1,9},{9,17},{17,25},{2,10},{10,18},{18,26},{... | collective-permute-start | bytes 12296 | tf_op jit(solution)/shard_map/ppermute | solution.py:46
  25.0 2.3 %half_rows.2 = f32[512,768]{1,0:T(8,128)} custom-call(f32[1024,1024]{1,0:T(8,128)} %refs_0_.1), custom_call_target="tpu_custom_call" | custom-call | tf_op jit(solution)/shard_map/half_rows/pallas_call | solution.py:216
  27.3 1.6 collective-permute-start.10
  29.4 23.1 %collective-permute-done.3.refs_0_ = f32[512,768]{1,0:T(8,128)S(1)} collective-permute-done((f32[512,768]{1,0:T(8,128)}, f32[512,768]{1,0:T(8,128)S(1)}, u32[]{:S(2)}, u32[]{:S(2)}) %collective-permute-start.3) | collective-permute-done | bytes 1572896 | tf_op jit(solution)/shard_map/ppermute | solution.py:229
  52.5 1.7 collective-permute-start.6
  54.2 10.6 %partial_jumps.2 = (f32[4,1024,256]{2,1,0:T(8,128)S(1)}, f32[8,1024]{1,0:T(8,128)S(1)}) custom-call(s32[1]{0:T(128)} %bitcast.at, f32[1024,1024]{1,0:T(8,128)} %refs_0_.1, f32[8192,1024]{1,0:T(8,128)} %refs_3_.5), custom_call_target="tpu_custom_call" | custom-call | flops 6442450944 | bytes 25165824 | tf_op jit(solution)/shard_map/partial_jumps/pallas_call | solution.py:148
  64.8 2.0 %copy-done = f32[4,1024,256]{2,1,0:T(8,128)} copy-done((f32[4,1024,256]{2,1,0:T(8,128)}, f32[4,1024,256]{2,1,0:T(8,128)S(1)}, u32[]{:S(2)}) %copy-start) | copy-done | bytes 4194328
  66.8 1.0 copy.10
  67.9 1.0 copy.11
  68.9 28.4 %collective-permute-done.refs_2_ = f32[512,768]{1,0:T(8,128)S(1)} collective-permute-done((f32[512,768]{1,0:T(8,128)}, f32[512,768]{1,0:T(8,128)S(1)}, u32[]{:S(2)}, u32[]{:S(2)}) %collective-permute-start) | collective-permute-done | bytes 1572896 | tf_op jit(solution)/shard_map/ppermute | solution.py:229
  97.3 1.5 collective-permute-start.4
  98.8 0.6 collective-permute-start.1
  99.4 11.8 %fusion.4.refs_6_ = f32[1024,1024]{1,0:T(8,128)} fusion(f32[1024,1024]{1,0:T(8,128)} %refs_0_.1, f32[1024,1]{1,0:T(8,128)} %copy.10, f32[1024,1]{1,0:T(8,128)} %copy.11, f32[1024]{0:T(1024)S(1)} %get-tuple-element.24, f32[1024]{0:T(1024)S(1)} %get-tuple-element.21, f32[1024]{0:T(1024)S(1)} %get-tuple-element.22, f32[1024]{0:T(1024)S(1)} %get-tuple-element.23, ...), kind=kLoop, calls=%fused_computation.5 | loop fusion | flops 33554432 | bytes 8417280 | tf_op jit(solution)/shard_map/add | solution.py:55
  111.3 1.8 fusion.7
  113.6 16.9 %add_jumps.5.refs_8_ = f32[1024,1024]{1,0:T(8,128)} custom-call(s32[1]{0:T(128)} %bitcast.at, f32[1024,1024]{1,0:T(8,128)} %refs_0_.1, f32[1024,1024]{1,0:T(8,128)} %collective-permute-done.12.refs_1_, f32[8192,1024]{1,0:T(8,128)} %refs_3_.5, f32[8192,1024]{1,0:T(8,128)} %refs_3_.5, f32[4,1024,256]{2,1,0:T(8,128)S(1)} %copy-done.1, ...), custom_call_target="tpu_custom_call", output_to_operand_aliasing={{}: (7, {})} | custom-call | flops 9663676416 | bytes 20971520 | tf_op jit(solution)/shard_map/add_jumps/pallas_call | solution.py:109
  130.6 1.9 collective-permute-done.4.refs_0_
  132.5 3.2 %collective-permute-done.1.refs_0_ = f32[512,768]{1,0:T(8,128)S(1)} collective-permute-done((f32[512,768]{1,0:T(8,128)S(1)}, f32[512,768]{1,0:T(8,128)S(1)}, u32[]{:S(2)}, u32[]{:S(2)}) %collective-permute-start.1) | collective-permute-done | bytes 1572896 | tf_op jit(solution)/shard_map/ppermute | solution.py:229
  136.2 15.2 %add_jumps.6.refs_8_ = f32[1024,1024]{1,0:T(8,128)} custom-call(s32[1]{0:T(128)} %bitcast.at, f32[512,768]{1,0:T(8,128)S(1)} %collective-permute-done.3.refs_0_, f32[512,768]{1,0:T(8,128)S(1)} %collective-permute-done.9.refs_1_, f32[512,768]{1,0:T(8,128)} %collective-permute-done.10.refs_2_, ...), custom_call_target="tpu_custom_call", output_to_operand_aliasing={{}: (9, {})} | custom-call | flops 9663676416 | bytes 20971520 | tf_op jit(solution)/shard_map/add_jumps/pallas_call | solution.py:109
  151.4 1.5 collective-permute-start.18
  153.4 15.2 %add_jumps.7.refs_4_ = f32[1024,1024]{1,0:T(8,128)} custom-call(s32[1]{0:T(128)} %bitcast.at, f32[512,768]{1,0:T(8,128)} %collective-permute-done.6.refs_0_, f32[512,768]{1,0:T(8,128)S(1)} %collective-permute-done.7.refs_1_, f32[512,768]{1,0:T(8,128)S(1)} %collective-permute-done.refs_2_, ...), custom_call_target="tpu_custom_call", output_to_operand_aliasing={{}: (9, {})} | custom-call | flops 9663676416 | bytes 20971520 | tf_op jit(solution)/shard_map/add_jumps/pallas_call | solution.py:109
  168.6 1.5 collective-permute-start.17
  170.1 1.4 fusion.9
  172.5 8.9 %add_jumps.8.refs_4_ = f32[1024,1024]{1,0:T(8,128)} custom-call(s32[1]{0:T(128)} %bitcast.at, f32[512,768]{1,0:T(8,128)S(1)} %collective-permute-done.4.refs_0_, f32[512,768]{1,0:T(8,128)S(1)} %collective-permute-done.5.refs_1_, f32[8192,1024]{1,0:T(8,128)} %refs_3_.5, f32[8192,1024]{1,0:T(8,128)} %refs_3_.5, ...), custom_call_target="tpu_custom_call", output_to_operand_aliasing={{}: (5, {})} | custom-call | flops 4831838208 | bytes 13631488 | tf_op jit(solution)/shard_map/add_jumps/pallas_call | solution.py:109
  181.4 8.9 %add_jumps.9.old = f32[1024,1024]{1,0:T(8,128)} custom-call(s32[1]{0:T(128)} %bitcast.at, f32[512,768]{1,0:T(8,128)S(1)} %collective-permute-done.1.refs_0_, f32[512,768]{1,0:T(8,128)S(1)} %collective-permute-done.2.refs_1_, f32[8192,1024]{1,0:T(8,128)} %refs_3_.5, f32[8192,1024]{1,0:T(8,128)} %refs_3_.5, ...), custom_call_target="tpu_custom_call", output_to_operand_aliasing={{}: (5, {})} | custom-call | flops 4831838208 | bytes 13631488 | tf_op jit(solution)/shard_map/add_jumps/pallas_call | solution.py:109
  190.3 1.4 slice_add_fusion.first
  191.7 1.6 collective-permute-done.19.combined_a
  193.3 1.1 add_last.1
  (40 shorter events, 3.9 us)
Async XLA Ops:
  11.8 87.0 %collective-permute-start.13 = (f32[4,1024,256]{2,1,0:T(8,128)}, f32[4,1024,256]{2,1,0:T(8,128)}, u32[]{:S(2)}, u32[]{:S(2)}) collective-permute-start(f32[4,1024,256]{2,1,0:T(8,128)} %get-tuple-element.10), channel_id=1, source_target_pairs={{0,1},{1,0},{2,3},{3,2},{4,5},{5,4},{6,7},{7,6},{8,9},{9,8},{10,11... | collective-permute-start | bytes 12582920 | tf_op jit(solution)/shard_map/ppermute | solution.py:229
  14.6 37.8 %collective-permute-start.3 = (f32[512,768]{1,0:T(8,128)}, f32[512,768]{1,0:T(8,128)S(1)}, u32[]{:S(2)}, u32[]{:S(2)}) collective-permute-start(f32[512,768]{1,0:T(8,128)} %half_rows.3), channel_id=1, source_target_pairs={{0,2},{1,3},{2,0},{3,1},{4,6},{5,7},{6,4},{7,5},{8,10},{9,11},{10,... | collective-permute-start | bytes 4718600 | tf_op jit(solution)/shard_map/ppermute | solution.py:229
  17.2 96.1 %collective-permute-start.12 = (f32[1024,1024]{1,0:T(8,128)}, f32[1024,1024]{1,0:T(8,128)}, u32[]{:S(2)}, u32[]{:S(2)}) collective-permute-start(f32[1024,1024]{1,0:T(8,128)} %refs_0_.1), channel_id=1, source_target_pairs={{0,1},{1,0},{2,3},{3,2},{4,5},{5,4},{6,7},{7,6},{8,9},{9,8},{10,11... | collective-permute-start | bytes 12582920 | tf_op jit(solution)/shard_map/ppermute | solution.py:229
  19.1 8.2 %collective-permute-start.14 = (f32[1024]{0:T(1024)S(1)}, f32[1024]{0:T(1024)S(1)}, u32[]{:S(2)}, u32[]{:S(2)}) collective-permute-start(f32[1024]{0:T(1024)S(1)} %get-tuple-element.13), channel_id=1, source_target_pairs={{8,0},{16,8},{24,16},{9,1},{17,9},{25,17},{10,2},{18,10},{26,18},{... | collective-permute-start | bytes 12296 | tf_op jit(solution)/shard_map/ppermute | solution.py:47
  20.4 8.5 %collective-permute-start.15 = (f32[1024]{0:T(1024)S(1)}, f32[1024]{0:T(1024)S(1)}, u32[]{:S(2)}, u32[]{:S(2)}) collective-permute-start(f32[1024]{0:T(1024)S(1)} %get-tuple-element.14), channel_id=1, source_target_pairs={{0,8},{8,16},{16,24},{1,9},{9,17},{17,25},{2,10},{10,18},{18,26},{... | collective-permute-start | bytes 12296 | tf_op jit(solution)/shard_map/ppermute | solution.py:46
  27.3 41.6 %collective-permute-start.10 = (f32[512,768]{1,0:T(8,128)}, f32[512,768]{1,0:T(8,128)}, u32[]{:S(2)}, u32[]{:S(2)}) collective-permute-start(f32[512,768]{1,0:T(8,128)} %half_rows.3), channel_id=1, source_target_pairs={{0,4},{1,5},{2,6},{3,7},{4,0},{5,1},{6,2},{7,3},{8,12},{9,13},{10,... | collective-permute-start | bytes 4718600 | tf_op jit(solution)/shard_map/ppermute | solution.py:229
  28.9 68.4 %collective-permute-start = (f32[512,768]{1,0:T(8,128)}, f32[512,768]{1,0:T(8,128)S(1)}, u32[]{:S(2)}, u32[]{:S(2)}) collective-permute-start(f32[512,768]{1,0:T(8,128)} %half_rows.2), channel_id=1, source_target_pairs={{0,4},{1,5},{2,6},{3,7},{4,0},{5,1},{6,2},{7,3},{8,12},{9,13},{10,... | collective-permute-start | bytes 4718600 | tf_op jit(solution)/shard_map/ppermute | solution.py:229
  52.5 46.4 %collective-permute-start.6 = (f32[512,768]{1,0:T(8,128)}, f32[512,768]{1,0:T(8,128)}, u32[]{:S(2)}, u32[]{:S(2)}) collective-permute-start(f32[512,768]{1,0:T(8,128)} %half_rows.2), channel_id=1, source_target_pairs={{0,2},{1,3},{2,0},{3,1},{4,6},{5,7},{6,4},{7,5},{8,10},{9,11},{10,... | collective-permute-start | bytes 4718600 | tf_op jit(solution)/shard_map/ppermute | solution.py:229
  54.2 13.6 %copy-start.2 = (f32[1024]{0:T(1024)S(1)}, f32[1024]{0:T(1024)}, u32[]{:S(2)}) copy-start(f32[1024]{0:T(1024)} %param.4) | copy-start | bytes 12292
  64.8 2.0 %copy-start = (f32[4,1024,256]{2,1,0:T(8,128)}, f32[4,1024,256]{2,1,0:T(8,128)S(1)}, u32[]{:S(2)}) copy-start(f32[4,1024,256]{2,1,0:T(8,128)S(1)} %get-tuple-element.9.refs_4_) | copy-start | bytes 12582916
  68.9 44.2 %collective-permute-start.9 = (f32[512,768]{1,0:T(8,128)S(1)}, f32[512,768]{1,0:T(8,128)S(1)}, u32[]{:S(2)}, u32[]{:S(2)}) collective-permute-start(f32[512,768]{1,0:T(8,128)S(1)} %collective-permute-done.3.refs_0_), channel_id=1, source_target_pairs={{0,1},{1,0},{2,3},{3,2},{4,5},{5,4},{6,7},{7,6},{8,9},{9,8},{10,11... | collective-permute-start | bytes 4718600 | tf_op jit(solution)/shard_map/ppermute | solution.py:229
  97.3 35.2 %collective-permute-start.4 = (f32[512,768]{1,0:T(8,128)S(1)}, f32[512,768]{1,0:T(8,128)S(1)}, u32[]{:S(2)}, u32[]{:S(2)}) collective-permute-start(f32[512,768]{1,0:T(8,128)S(1)} %collective-permute-done.3.refs_0_), channel_id=1, source_target_pairs={{0,4},{1,5},{2,6},{3,7},{4,0},{5,1},{6,2},{7,3},{8,12},{9,13},{10,... | collective-permute-start | bytes 4718600 | tf_op jit(solution)/shard_map/ppermute | solution.py:229
  98.8 36.8 %collective-permute-start.11 = (f32[512,768]{1,0:T(8,128)}, f32[512,768]{1,0:T(8,128)S(1)}, u32[]{:S(2)}, u32[]{:S(2)}) collective-permute-start(f32[512,768]{1,0:T(8,128)} %collective-permute-done.10.refs_2_), channel_id=1, source_target_pairs={{0,1},{1,0},{2,3},{3,2},{4,5},{5,4},{6,7},{7,6},{8,9},{9,8},{10,11... | collective-permute-start | bytes 4718600 | tf_op jit(solution)/shard_map/ppermute | solution.py:229
  98.8 36.8 %collective-permute-start.1 = (f32[512,768]{1,0:T(8,128)S(1)}, f32[512,768]{1,0:T(8,128)S(1)}, u32[]{:S(2)}, u32[]{:S(2)}) collective-permute-start(f32[512,768]{1,0:T(8,128)S(1)} %collective-permute-done.refs_2_), channel_id=1, source_target_pairs={{0,2},{1,3},{2,0},{3,1},{4,6},{5,7},{6,4},{7,5},{8,10},{9,11},{10,... | collective-permute-start | bytes 4718600 | tf_op jit(solution)/shard_map/ppermute | solution.py:229
  99.4 11.8 %copy-start.1 = (f32[4,1024,256]{2,1,0:T(8,128)S(1)}, f32[4,1024,256]{2,1,0:T(8,128)}, u32[]{:S(2)}) copy-start(f32[4,1024,256]{2,1,0:T(8,128)} %copy-done) | copy-start | bytes 12582916
  113.1 38.3 %collective-permute-start.8 = (f32[512,768]{1,0:T(8,128)S(1)}, f32[512,768]{1,0:T(8,128)S(1)}, u32[]{:S(2)}, u32[]{:S(2)}) collective-permute-start(f32[512,768]{1,0:T(8,128)S(1)} %collective-permute-done.refs_2_), channel_id=1, source_target_pairs={{0,1},{1,0},{2,3},{3,2},{4,5},{5,4},{6,7},{7,6},{8,9},{9,8},{10,11... | collective-permute-start | bytes 4718600 | tf_op jit(solution)/shard_map/ppermute | solution.py:229
  113.3 39.6 %collective-permute-start.7 = (f32[512,768]{1,0:T(8,128)}, f32[512,768]{1,0:T(8,128)S(1)}, u32[]{:S(2)}, u32[]{:S(2)}) collective-permute-start(f32[512,768]{1,0:T(8,128)} %collective-permute-done.6.refs_0_), channel_id=1, source_target_pairs={{0,1},{1,0},{2,3},{3,2},{4,5},{5,4},{6,7},{7,6},{8,9},{9,8},{10,11... | collective-permute-start | bytes 4718600 | tf_op jit(solution)/shard_map/ppermute | solution.py:229
  132.5 39.6 %collective-permute-start.5 = (f32[512,768]{1,0:T(8,128)S(1)}, f32[512,768]{1,0:T(8,128)S(1)}, u32[]{:S(2)}, u32[]{:S(2)}) collective-permute-start(f32[512,768]{1,0:T(8,128)S(1)} %collective-permute-done.4.refs_0_), channel_id=1, source_target_pairs={{0,1},{1,0},{2,3},{3,2},{4,5},{5,4},{6,7},{7,6},{8,9},{9,8},{10,11... | collective-permute-start | bytes 4718600 | tf_op jit(solution)/shard_map/ppermute | solution.py:229
  135.6 45.8 %collective-permute-start.2 = (f32[512,768]{1,0:T(8,128)S(1)}, f32[512,768]{1,0:T(8,128)S(1)}, u32[]{:S(2)}, u32[]{:S(2)}) collective-permute-start(f32[512,768]{1,0:T(8,128)S(1)} %collective-permute-done.1.refs_0_), channel_id=1, source_target_pairs={{0,1},{1,0},{2,3},{3,2},{4,5},{5,4},{6,7},{7,6},{8,9},{9,8},{10,11... | collective-permute-start | bytes 4718600 | tf_op jit(solution)/shard_map/ppermute | solution.py:229
  135.6 54.7 %collective-permute-start.16 = (f32[512,256]{1,0:T(8,128)S(1)}, f32[512,256]{1,0:T(8,128)S(1)}, u32[]{:S(2)}, u32[]{:S(2)}) collective-permute-start(f32[512,256]{1,0:T(8,128)S(1)} %get-tuple-element.20), channel_id=1, source_target_pairs={{0,2},{1,3},{2,0},{3,1},{4,6},{5,7},{6,4},{7,5},{8,10},{9,11},{10,... | collective-permute-start | bytes 1572872 | tf_op jit(solution)/shard_map/ppermute | solution.py:229
  151.4 17.2 %collective-permute-start.18 = (f32[512,256]{1,0:T(8,128)S(1)}, f32[512,256]{1,0:T(8,128)S(1)}, u32[]{:S(2)}, u32[]{:S(2)}) collective-permute-start(f32[512,256]{1,0:T(8,128)S(1)} %get-tuple-element.18), channel_id=1, source_target_pairs={{0,2},{1,3},{2,0},{3,1},{4,6},{5,7},{6,4},{7,5},{8,10},{9,11},{10,... | collective-permute-start | bytes 1572872 | tf_op jit(solution)/shard_map/ppermute | solution.py:229
  152.9 17.2 %collective-permute-start.20 = (f32[512,256]{1,0:T(8,128)S(1)}, f32[512,256]{1,0:T(8,128)S(1)}, u32[]{:S(2)}, u32[]{:S(2)}) collective-permute-start(f32[512,256]{1,0:T(8,128)S(1)} %get-tuple-element.17), channel_id=1, source_target_pairs={{0,4},{1,5},{2,6},{3,7},{4,0},{5,1},{6,2},{7,3},{8,12},{9,13},{10,... | collective-permute-start | bytes 1572872 | tf_op jit(solution)/shard_map/ppermute | solution.py:229
  168.6 21.7 %collective-permute-start.17 = (f32[512,256]{1,0:T(8,128)S(1)}, f32[512,256]{1,0:T(8,128)S(1)}, u32[]{:S(2)}, u32[]{:S(2)}) collective-permute-start(f32[512,256]{1,0:T(8,128)S(1)} %get-tuple-element.19), channel_id=1, source_target_pairs={{0,4},{1,5},{2,6},{3,7},{4,0},{5,1},{6,2},{7,3},{8,12},{9,13},{10,... | collective-permute-start | bytes 1572872 | tf_op jit(solution)/shard_map/ppermute | solution.py:229
  171.5 21.8 %collective-permute-start.19 = (f32[512,256]{1,0:T(8,128)S(1)}, f32[512,256]{1,0:T(8,128)S(1)}, u32[]{:S(2)}, u32[]{:S(2)}) collective-permute-start(f32[512,256]{1,0:T(8,128)S(1)} %get-tuple-element.16), channel_id=1, source_target_pairs={{0,4},{1,5},{2,6},{3,7},{4,0},{5,1},{6,2},{7,3},{8,12},{9,13},{10,... | collective-permute-start | bytes 1572872 | tf_op jit(solution)/shard_map/ppermute | solution.py:229
  172.1 21.2 %collective-permute-start.21 = (f32[512,256]{1,0:T(8,128)S(1)}, f32[512,256]{1,0:T(8,128)S(1)}, u32[]{:S(2)}, u32[]{:S(2)}) collective-permute-start(f32[512,256]{1,0:T(8,128)S(1)} %get-tuple-element.15), channel_id=1, source_target_pairs={{0,2},{1,3},{2,0},{3,1},{4,6},{5,7},{6,4},{7,5},{8,10},{9,11},{10,... | collective-permute-start | bytes 1572872 | tf_op jit(solution)/shard_map/ppermute | solution.py:229
